TPU v7x, 512 devices: a whole 4x8x8 slice. The times are simulated.
512 devices in a mesh: leaf: 32 (over x, y), front: 16 (over z, core).
Axes of the slice: x: 4, y: 8, z: 8, core: 2. Of those that a mesh axis runs over, the one named last changes fastest.
Arguments:
- coupling: bfloat16 [65536, 2048], P('leaf', 'front'), may hold values from -0.015625 to 0.015625
- block_pattern: int32 [32, 16, 16], P('leaf', None, 'front'), may hold values 0 or 1
- supernode_inverse: bfloat16 [512, 128, 128], P('leaf'), may hold values from -0.6 to 2, as said below
- subdomain_sizes: int32 [32], P('leaf'), may hold values from 512 to 2048, as said below
- block_maps: int32 [4, 32, 16], P(None, 'leaf'), may hold values from 0 to 15, as said below
- top_fronts: float32 [2, 2048, 2048], P(None, None, 'front'), may hold values from -108 to 140
Outputs:
- factored_fronts: float32 [4096, 2048], P('leaf', 'front')
Inputs may be any that keep to these rules, and one draw needn't show every extreme that they name: `subdomain_sizes`: uneven interior sizes; some subdomain has exactly 2048. block_maps[k, l] is the map of the level-k tree node holding subdomain l (subdomains with equal l // 2**k share it, and its row): a permutation of 0 .. 15 sending the node's separator block b to block block_maps[k, l, b] of its parent's. `supernode_inverse`: each block is lower triangular with its diagonal between 1 and 2.
All inputs are finite; a program needn't handle non-finite values. No bound on the sum of `block_pattern` on one device may be relied on, other than what follows from the above.
Results may differ from a plain program's by a relative error of at most 0.00085.
Values may be sent and summed in bfloat16 or wider, within the bound.
A program may use at most 128 MiB of HBM per device.

v0:
```python
import jax
import jax.numpy as jnp
from jax import lax
from jax.sharding import PartitionSpec as P

PIV = 512


def from_partner(value, axis, bit):
    mask = 2**bit
    pairs = [(source, source ^ mask) for source in range(lax.axis_size(axis))]
    return lax.ppermute(value, axis, pairs)


def spread(value, axis, root):
    mine = lax.axis_index(axis) == root
    return lax.psum(jnp.where(mine, value, jnp.zeros_like(value)), axis)


def solve_lower(factor, rhs_rows):
    return jax.scipy.linalg.solve_triangular(factor, rhs_rows, lower=True)


def shards(coupling, block_pattern, supernode_inverse, subdomain_sizes, block_maps, top_fronts):
    leaf_count = lax.axis_size("leaf")
    leaf_index = lax.axis_index("leaf")
    front_index = lax.axis_index("front")
    levels = block_maps.shape[0]
    group_size = leaf_count // top_fronts.shape[0]
    row_count, col_count = coupling.shape
    block_size = supernode_inverse.shape[1]
    row_blocks = row_count // block_size
    col_blocks = col_count // block_size
    front_order = top_fronts.shape[1]
    front_blocks = front_order // block_size
    pattern_scale = block_pattern[0].astype(jnp.bfloat16)[:, None, :, None]
    masked = (
        coupling.reshape(row_blocks, block_size, col_blocks, block_size) * pattern_scale
    ).reshape(row_blocks, block_size, col_count)
    solved = jnp.einsum(
        "rab,rbc->rac", supernode_inverse, masked, preferred_element_type=jnp.float32
    )
    live_rows = (jnp.arange(row_count) < subdomain_sizes[0]).reshape(row_blocks, block_size, 1)
    panel_cols = (
        jnp.where(live_rows, solved, 0.0).astype(jnp.bfloat16).reshape(row_count, col_count)
    )
    gathered = lax.all_gather(panel_cols, "front", axis=1, tiled=True)
    positions = jnp.arange(front_blocks)
    composite = block_maps[0, 0]
    for merge_level in range(1, levels):
        level_map = block_maps[merge_level, 0]
        composite = jnp.sum(
            jnp.where(composite[:, None] == positions[None, :], level_map[None, :], 0), axis=1
        )
    inverse = jnp.sum(
        jnp.where(composite[:, None] == positions[None, :], positions[:, None], 0), axis=0
    )
    sources = lax.dynamic_slice_in_dim(inverse, front_index * col_blocks, col_blocks)
    selected = gathered.reshape(row_count, front_blocks, block_size)[:, sources, :].reshape(
        row_count, col_count
    )
    products = jnp.einsum("nk,nc->kc", gathered, selected, preferred_element_type=jnp.float32)
    summed = -products.reshape(front_blocks, block_size, col_count)[inverse].reshape(
        front_order, col_count
    )
    for merge_level in range(levels):
        summed = summed + from_partner(summed.astype(jnp.bfloat16), "leaf", merge_level).astype(
            summed.dtype
        )
    top_index = leaf_index // group_size
    column = lax.dynamic_index_in_dim(top_fronts, top_index, 0, keepdims=False) + summed
    pivot_blocks = PIV // col_count
    for pivot_step in range(pivot_blocks):
        row_start = pivot_step * col_count
        diag_factor = jnp.linalg.cholesky(column[row_start : row_start + col_count])
        below_rows = solve_lower(diag_factor, column[row_start + col_count :].T).T
        candidate = jnp.concatenate([diag_factor, below_rows])
        shared = spread(candidate, "front", pivot_step)
        offset = jnp.clip(
            front_index * col_count - row_start, 0, front_order - row_start - col_count
        )
        partner_rows = lax.dynamic_slice_in_dim(shared, offset, col_count)
        change = jnp.dot(
            shared,
            partner_rows.T,
            precision=lax.Precision.HIGHEST,
            preferred_element_type=jnp.float32,
        )
        tail_rows = jnp.where(
            front_index > pivot_step, column[row_start:] - change, column[row_start:]
        )
        tail_rows = jnp.where(front_index == pivot_step, shared, tail_rows)
        head_rows = jnp.where(front_index == pivot_step, 0.0, column[:row_start])
        column = jnp.concatenate([head_rows, tail_rows])
    zero_top = jnp.concatenate([jnp.zeros((PIV, col_count), jnp.float32), column[PIV:]])
    column = jnp.where(front_index >= pivot_blocks, zero_top, column)
    rows_each = front_order // group_size
    return lax.dynamic_slice_in_dim(column, leaf_index % group_size * rows_each, rows_each)


def solution(mesh):
    return jax.shard_map(
        shards,
        mesh=mesh,
        in_specs=(
            P("leaf", "front"),
            P("leaf", None, "front"),
            P("leaf", None, None),
            P("leaf"),
            P(None, "leaf", None),
            P(None, None, "front"),
        ),
        out_specs=P("leaf", "front"),
        check_vma=False,
    )
```

profile of v0, /device:TPU:7, one launch (start us, length us, event | category | flops | bytes accessed | tf_op | source)
XLA Modules:
  0.0 790.0 jit_solution(483369339221364038)
XLA Ops:
  7.3 0.7 convert_bitcast_fusion
  7.9 2.3 fusion.8
  10.3 0.7 slice_bitcast_fusion.3
  11.0 0.2 select_reduce_fusion.4
  11.2 0.2 select_reduce_fusion.3
  11.4 0.2 select_reduce_fusion.2
  11.6 0.1 select_reduce_fusion.1
  11.6 0.6 dynamic_slice.23
  14.2 68.6 %all-gather.2.cloned.1.call-done = bf16[2048,2048]{1,0:T(8,128)(2,1)} async-done(((bf16[2048,128]{1,0:T(8,128)(2,1)}), bf16[2048,2048]{1,0:T(8,128)(2,1)}) %all-gather.2.cloned.1.call-update) | async-done | bytes 8388624 | tf_op jit(solution)/shard_map/all_gather | solution.py:47
  82.8 9.8 %copy.28 = bf16[256,8,16,128]{3,2,1,0:T(8,128)(2,1)} copy(bf16[256,8,16,128]{3,1,2,0:T(8,128)(2,1)} %bitcast.84) | data formatting | bytes 16777216
  92.6 12.3 %copy.17 = bf16[2048,2048]{1,0:T(8,128)(2,1)} copy(bf16[2048,2048]{0,1:T(8,128)(2,1)} %bitcast.85) | data formatting | bytes 16777216 | tf_op jit(solution)/shard_map/nk,nc->kc/dot_general | solution.py:62
  104.9 2.8 constant_dynamic-slice_fusion
  107.7 5.8 fusion.18
  113.5 0.6 gather_fusion
  114.1 0.1 neg.6
  114.2 3.1 collective-permute-start
  117.3 12.0 %collective-permute-done = bf16[2048,128]{1,0:T(8,128)(2,1)S(1)} collective-permute-done((bf16[2048,128]{1,0:T(8,128)(2,1)S(1)}, bf16[2048,128]{1,0:T(8,128)(2,1)S(1)}, u32[]{:S(2)}, u32[]{:S(2)}) %collective-permute-start) | collective-permute-done | bytes 524320 | tf_op jit(solution)/shard_map/ppermute | solution.py:12
  129.4 0.1 fusion.24
  129.5 4.0 collective-permute-start.1
  133.5 22.9 %collective-permute-done.1 = bf16[2048,128]{1,0:T(8,128)(2,1)S(1)} collective-permute-done((bf16[2048,128]{1,0:T(8,128)(2,1)S(1)}, bf16[2048,128]{1,0:T(8,128)(2,1)S(1)}, u32[]{:S(2)}, u32[]{:S(2)}) %collective-permute-start.1) | collective-permute-done | bytes 524320 | tf_op jit(solution)/shard_map/ppermute | solution.py:12
  156.4 0.2 fusion.17
  156.6 8.0 %collective-permute-start.2 = (bf16[2048,128]{1,0:T(8,128)(2,1)S(1)}, bf16[2048,128]{1,0:T(8,128)(2,1)S(1)}, u32[]{:S(2)}, u32[]{:S(2)}) collective-permute-start(bf16[2048,128]{1,0:T(8,128)(2,1)S(1)} %fusion.17), channel_id=1, source_target_pairs={{0,64},{16,80},{32,96},{48,112},{64,0},{80,16},{96,32},{112,48},{1... | collective-permute-start | bytes 1572872 | tf_op jit(solution)/shard_map/ppermute | solution.py:12
  164.6 22.6 %collective-permute-done.2 = bf16[2048,128]{1,0:T(8,128)(2,1)S(1)} collective-permute-done((bf16[2048,128]{1,0:T(8,128)(2,1)S(1)}, bf16[2048,128]{1,0:T(8,128)(2,1)S(1)}, u32[]{:S(2)}, u32[]{:S(2)}) %collective-permute-start.2) | collective-permute-done | bytes 524320 | tf_op jit(solution)/shard_map/ppermute | solution.py:12
  187.2 1.1 fusion.20
  188.3 2.8 collective-permute-start.3
  191.1 11.2 %collective-permute-done.3 = bf16[2048,128]{1,0:T(8,128)(2,1)} collective-permute-done((bf16[2048,128]{1,0:T(8,128)(2,1)}, bf16[2048,128]{1,0:T(8,128)(2,1)}, u32[]{:S(2)}, u32[]{:S(2)}) %collective-permute-start.3) | collective-permute-done | bytes 524320 | tf_op jit(solution)/shard_map/ppermute | solution.py:12
  202.3 2.0 bitcast_add_fusion.1
  204.5 0.1 copy.20
  204.6 11.7 %cholesky.74 = f32[128,128]{1,0:T(8,128)S(1)} custom-call(f32[128,128]{1,0:T(8,128)S(1)} %copy.20), custom_call_target="Cholesky" | custom-call | tf_op jit(solution)/shard_map/jit(cholesky)/cholesky | solution.py:75
  216.3 0.6 compare_reduce_fusion.3
  216.9 0.7 fusion.48
  217.6 9.8 %custom-call.18 = f32[1,128,128]{1,2,0:T(8,128)S(1)} custom-call(f32[1,128,128]{2,1,0:T(8,128)S(1)} %get-tuple-element.23), custom_call_target="InvertDiagBlocksLowerTriangular" | custom-call | tf_op jit(solution)/shard_map/jit(_solve_triangular)/triangular_solve | solution.py:21
  227.4 0.9 fusion.9
  228.4 1.1 maximum_select_fusion
  229.5 0.6 all-reduce.8.cloned.1.call-start
  230.1 116.0 %all-reduce.6.cloned.1.call-done = f32[2048,128]{1,0:T(8,128)} async-done(((f32[2048,128]{1,0:T(8,128)}), f32[2048,128]{1,0:T(8,128)}) %all-reduce.6.cloned.1.call-update) | async-done | bytes 1048592 | tf_op jit(solution)/shard_map/psum | solution.py:17
  346.1 2.6 fusion.7
  348.9 11.7 %cholesky.85 = f32[128,128]{1,0:T(8,128)S(1)} custom-call(f32[128,128]{1,0:T(8,128)S(1)} %copy.22), custom_call_target="Cholesky" | custom-call | tf_op jit(solution)/shard_map/jit(cholesky)/cholesky | solution.py:75
  360.6 0.6 compare_reduce_fusion.2
  361.3 0.7 fusion.49
  362.0 9.8 %custom-call.19 = f32[1,128,128]{1,2,0:T(8,128)S(1)} custom-call(f32[1,128,128]{2,1,0:T(8,128)S(1)} %get-tuple-element.21), custom_call_target="InvertDiagBlocksLowerTriangular" | custom-call | tf_op jit(solution)/shard_map/jit(_solve_triangular)/triangular_solve | solution.py:21
  371.8 0.9 fusion.11
  372.6 1.0 maximum_select_fusion.1
  373.7 0.2 all-reduce.10.cloned.1.call-start
  373.9 116.7 %all-reduce.8.cloned.1.call-done = f32[1920,128]{1,0:T(8,128)} async-done(((f32[1920,128]{1,0:T(8,128)}), f32[1920,128]{1,0:T(8,128)}) %all-reduce.8.cloned.1.call-update) | async-done | bytes 983056 | tf_op jit(solution)/shard_map/psum | solution.py:17
  490.6 2.8 fusion.5
  493.6 11.7 %cholesky.96 = f32[128,128]{1,0:T(8,128)S(1)} custom-call(f32[128,128]{1,0:T(8,128)S(1)} %copy.24), custom_call_target="Cholesky" | custom-call | tf_op jit(solution)/shard_map/jit(cholesky)/cholesky | solution.py:75
  505.4 0.6 compare_reduce_fusion.1
  506.0 0.7 fusion.50
  506.7 9.8 %custom-call.20 = f32[1,128,128]{1,2,0:T(8,128)S(1)} custom-call(f32[1,128,128]{2,1,0:T(8,128)S(1)} %get-tuple-element.19), custom_call_target="InvertDiagBlocksLowerTriangular" | custom-call | tf_op jit(solution)/shard_map/jit(_solve_triangular)/triangular_solve | solution.py:21
  516.5 0.8 fusion.13
  517.3 1.0 maximum_select_fusion.2
  518.4 0.3 all-reduce.12.cloned.1.call-start
  518.6 117.8 %all-reduce.10.cloned.1.call-done = f32[1792,128]{1,0:T(8,128)} async-done(((f32[1792,128]{1,0:T(8,128)}), f32[1792,128]{1,0:T(8,128)}) %all-reduce.10.cloned.1.call-update) | async-done | bytes 917520 | tf_op jit(solution)/shard_map/psum | solution.py:17
  636.4 2.4 fusion.3
  639.0 11.7 %cholesky.107 = f32[128,128]{1,0:T(8,128)S(1)} custom-call(f32[128,128]{1,0:T(8,128)S(1)} %copy.26), custom_call_target="Cholesky" | custom-call | tf_op jit(solution)/shard_map/jit(cholesky)/cholesky | solution.py:75
  650.8 0.6 compare_reduce_fusion
  651.4 0.7 fusion.51
  652.1 9.8 %custom-call.21 = f32[1,128,128]{1,2,0:T(8,128)S(1)} custom-call(f32[1,128,128]{2,1,0:T(8,128)S(1)} %get-tuple-element.17), custom_call_target="InvertDiagBlocksLowerTriangular" | custom-call | tf_op jit(solution)/shard_map/jit(_solve_triangular)/triangular_solve | solution.py:21
  661.9 0.8 fusion.15
  662.7 1.0 maximum_select_fusion.3
  663.8 116.4 %all-reduce.12.cloned.1.call-done = f32[1664,128]{1,0:T(8,128)} async-done(((f32[1664,128]{1,0:T(8,128)}), f32[1664,128]{1,0:T(8,128)}) %all-reduce.12.cloned.1.call-update) | async-done | bytes 851984 | tf_op jit(solution)/shard_map/psum | solution.py:17
  780.2 2.3 fusion.1
  782.5 0.7 fusion.25
  (41 shorter events, 1.1 us)
Async XLA Ops:
  6.5 1.4 copy-start
  6.5 76.3 %all-gather.2.cloned.1.call-start = ((), (), s32[]{:S(2)}) async-start(), calls=%async_computation | async-start | bytes 8912896 | tf_op jit(solution)/shard_map/all_gather | solution.py:47
  10.2 335.8 %all-reduce.6.cloned.1.call-start = ((), (), s32[]{:S(2)}) async-start(), calls=%async_computation.1 | async-start | bytes 2097152 | tf_op jit(solution)/shard_map/psum | solution.py:17
  114.2 15.1 %collective-permute-start = (bf16[2048,128]{1,0:T(8,128)(2,1)S(1)}, bf16[2048,128]{1,0:T(8,128)(2,1)S(1)}, u32[]{:S(2)}, u32[]{:S(2)}) collective-permute-start(bf16[2048,128]{1,0:T(8,128)(2,1)S(1)} %bitcast_convert_fusion), channel_id=1, source_target_pairs={{0,16},{16,0},{32,48},{48,32},{64,80},{80,64},{96,112},{112,96},{1... | collective-permute-start | bytes 1572872 | tf_op jit(solution)/shard_map/ppermute | solution.py:12
  129.5 27.0 %collective-permute-start.1 = (bf16[2048,128]{1,0:T(8,128)(2,1)S(1)}, bf16[2048,128]{1,0:T(8,128)(2,1)S(1)}, u32[]{:S(2)}, u32[]{:S(2)}) collective-permute-start(bf16[2048,128]{1,0:T(8,128)(2,1)S(1)} %fusion.24), channel_id=1, source_target_pairs={{0,32},{16,48},{32,0},{48,16},{64,96},{80,112},{96,64},{112,80},{1... | collective-permute-start | bytes 1572872 | tf_op jit(solution)/shard_map/ppermute | solution.py:12
  156.4 34.7 %copy-start.2 = (bf16[2048,128]{1,0:T(8,128)(2,1)}, bf16[2048,128]{1,0:T(8,128)(2,1)S(1)}, u32[]{:S(2)}) copy-start(bf16[2048,128]{1,0:T(8,128)(2,1)S(1)} %collective-permute-done.1) | copy-start | bytes 1572868
  156.6 30.6 %collective-permute-start.2 = (bf16[2048,128]{1,0:T(8,128)(2,1)S(1)}, bf16[2048,128]{1,0:T(8,128)(2,1)S(1)}, u32[]{:S(2)}, u32[]{:S(2)}) collective-permute-start(bf16[2048,128]{1,0:T(8,128)(2,1)S(1)} %fusion.17), channel_id=1, source_target_pairs={{0,64},{16,80},{32,96},{48,112},{64,0},{80,16},{96,32},{112,48},{1... | collective-permute-start | bytes 1572872 | tf_op jit(solution)/shard_map/ppermute | solution.py:12
  187.2 3.9 copy-start.3
  188.3 14.1 %collective-permute-start.3 = (bf16[2048,128]{1,0:T(8,128)(2,1)}, bf16[2048,128]{1,0:T(8,128)(2,1)}, u32[]{:S(2)}, u32[]{:S(2)}) collective-permute-start(bf16[2048,128]{1,0:T(8,128)(2,1)} %fusion.20), channel_id=1, source_target_pairs={{0,128},{16,144},{32,160},{48,176},{64,192},{80,208},{96,224},{112... | collective-permute-start | bytes 1572872 | tf_op jit(solution)/shard_map/ppermute | solution.py:12
  229.5 261.1 %all-reduce.8.cloned.1.call-start = ((), (), s32[]{:S(2)}) async-start(), calls=%async_computation.2 | async-start | bytes 1966080 | tf_op jit(solution)/shard_map/psum | solution.py:17
  348.6 25.3 %copy-start.1 = (f32[2048,128]{1,0:T(8,128)}, f32[2048,128]{1,0:T(8,128)S(1)}, u32[]{:S(2)}) copy-start(f32[2048,128]{1,0:T(8,128)S(1)} %fusion.7) | copy-start | bytes 3145732
  373.7 262.8 %all-reduce.10.cloned.1.call-start = ((), (), s32[]{:S(2)}) async-start(), calls=%async_computation.3 | async-start | bytes 1835008 | tf_op jit(solution)/shard_map/psum | solution.py:17
  518.4 261.8 %all-reduce.12.cloned.1.call-start = ((), (), s32[]{:S(2)}) async-start(), calls=%async_computation.4 | async-start | bytes 1703936 | tf_op jit(solution)/shard_map/psum | solution.py:17
Sparse Core Ops, SparseCore 0:
  10.4 72.4 all-gather.1
  229.6 116.4 all-reduce.5
  373.8 116.7 all-reduce.7
  518.5 117.9 all-reduce.9
  663.8 116.2 all-reduce.11
where the time goes:
time: 798 us; the launch traced here: 790 us
  waiting for transfers between devices  604 us (76%)
  other arithmetic  101 us (13%)
  local copies, waits for them, and re-layouts  27.6 us (3%)
  matrix products  21.4 us (3%)
  starting transfers between devices  19 us (2%)
  between operations  16.5 us (2%)
    psum x4, waiting for transfers between devices, spread(): return lax.psum(jnp.where(mine, value, jnp.zeros_like(value)), axis)  467 us
    ppermute x4, waiting for transfers between devices, from_partner(): return lax.ppermute(value, axis, pairs)  68.8 us
    all_gather x1, waiting for transfers between devices, shards(): gathered = lax.all_gather(panel_cols, 'front', axis=1, tiled=True)  68.6 us
    another operation x12, other arithmetic, shards(): diag_factor = jnp.linalg.cholesky(column[row_start:row_start + col_count])  49.6 us
    another operation x8, other arithmetic, solve_lower(): return jax.scipy.linalg.solve_triangular(factor, rhs_rows, lower=True)  41.9 us
    ppermute x4, starting transfers between devices, from_partner(): return lax.ppermute(value, axis, pairs)  17.9 us
  transfers between devices with their start and end apart: 9, of which 9 were waited for; matrix products, arithmetic and copies ran while one was open for 0% of the time, Pallas kernels for 0%

commit v1 on v0

v1 whole, which is shorter than its diff:
```python
import jax
import jax.numpy as jnp
from jax import lax
from jax.experimental import pallas as pl
from jax.experimental.pallas import tpu as pltpu
from jax.sharding import PartitionSpec as P

NN = (((1,), (0,)), ((), ()))
NT = (((1,), (1,)), ((), ()))
TN = (((0,), (0,)), ((), ()))


def halves(x):
    hi = x.astype(jnp.bfloat16)
    return hi, (x - hi.astype(jnp.float32)).astype(jnp.bfloat16)


def mm(a, b, dims):
    return lax.dot_general(a, b, dims, preferred_element_type=jnp.float32)


def mm3(a, b, dims):
    ah, al = halves(a)
    bh, bl = halves(b)
    return mm(ah, bh, dims) + (mm(ah, bl, dims) + mm(al, bh, dims))


def finish_kernel(index_ref, a_ref, ai_ref, aj_ref, aij_ref, out_ref, y_ref, w_ref):
    n = a_ref.shape[0]
    b = ai_ref.shape[1]
    rows = lax.broadcasted_iota(jnp.int32, (n, n), 0)
    cols = lax.broadcasted_iota(jnp.int32, (n, n), 1)
    eye = (rows == cols).astype(jnp.float32)
    weight = jnp.where(rows > cols, 1.0, jnp.where(rows == cols, 0.5, 0.0))
    diag = jnp.sum(a_ref[...] * eye, axis=0, keepdims=True)
    y_ref[...] = eye * lax.rsqrt(diag)

    def rough(_, carry):
        ab = a_ref[...].astype(jnp.bfloat16)
        yb = y_ref[...].astype(jnp.bfloat16)
        g = mm(ab, yb, NT).astype(jnp.bfloat16)
        e = (mm(yb, g, NN) - eye) * weight
        y_ref[...] = y_ref[...] - mm(e.astype(jnp.bfloat16), yb, NN)
        return carry

    lax.fori_loop(0, 2, rough, 0)

    def fine(carry):
        step, _ = carry
        y = y_ref[...]
        e = (mm3(y, mm3(a_ref[...], y, NT), NN) - eye) * weight
        y_ref[...] = y - mm3(e, y, NN)
        return step + 1, jnp.max(jnp.abs(e))

    def unfinished(carry):
        step, worst = carry
        return (step < 40) & jnp.logical_not(worst < 2e-3)

    _, worst = lax.while_loop(unfinished, fine, (jnp.int32(0), jnp.float32(1.0)))

    @pl.when(jnp.logical_not(worst < 2e-3))
    def _():
        w_ref[...] = a_ref[...]
        y_ref[...] = eye
        row_id = lax.broadcasted_iota(jnp.int32, (n, 1), 0)
        col_id = lax.broadcasted_iota(jnp.int32, (1, n), 1)

        def eliminate(k, carry):
            w = w_ref[...]
            y = y_ref[...]
            row = w_ref[pl.ds(k, 1), :]
            scale = lax.rsqrt(jnp.sum(jnp.where(col_id == k, row, 0.0)))
            row = row * scale
            row_y = y_ref[pl.ds(k, 1), :] * scale
            col = jnp.sum(jnp.where(col_id == k, w, 0.0), axis=1, keepdims=True) * scale
            below = jnp.where(row_id > k, col, 0.0)
            here = row_id == k
            w_ref[...] = jnp.where(here, row, w - below * row)
            y_ref[...] = jnp.where(here, row_y, y - below * row_y)
            return carry

        lax.fori_loop(0, n, eliminate, 0)

    block_row = index_ref[0]
    block_col = index_ref[1]
    pivots = n // b
    y = y_ref[...]
    xi = mm3(y, ai_ref[...], NN)
    xj = mm3(y, aj_ref[...], NN)
    schur = aij_ref[...] - mm3(xi, xj, TN)
    w_ref[:, :b] = xi
    picked = w_ref[pl.ds(pl.multiple_of(jnp.minimum(block_col, pivots - 1) * b, b), b), :b].T
    r = block_row * b + lax.broadcasted_iota(jnp.int32, (b, b), 0)
    c = block_col * b + lax.broadcasted_iota(jnp.int32, (b, b), 1)
    left = jnp.where(c <= r, picked, 0.0)
    right = jnp.where(block_row >= pivots, schur, 0.0)
    out_ref[...] = jnp.where(block_col >= pivots, right, left)


def finish(index, a, ai, aj, aij):
    n = a.shape[0]
    b = ai.shape[1]
    vmem = pl.BlockSpec(memory_space=pltpu.VMEM)
    return pl.pallas_call(
        finish_kernel,
        out_shape=jax.ShapeDtypeStruct((b, b), jnp.float32),
        in_specs=[pl.BlockSpec(memory_space=pltpu.SMEM)] + [vmem] * 4,
        out_specs=vmem,
        scratch_shapes=[pltpu.VMEM((n, n), jnp.float32), pltpu.VMEM((n, n), jnp.float32)],
    )(index, a, ai, aj, aij)

PIV = 512


def from_partner(value, axis, bit):
    mask = 2**bit
    pairs = [(source, source ^ mask) for source in range(lax.axis_size(axis))]
    return lax.ppermute(value, axis, pairs)


def shards(coupling, block_pattern, supernode_inverse, subdomain_sizes, block_maps, top_fronts):
    leaf_count = lax.axis_size("leaf")
    leaf_index = lax.axis_index("leaf")
    front_index = lax.axis_index("front")
    levels = block_maps.shape[0]
    group_size = leaf_count // top_fronts.shape[0]
    row_count, col_count = coupling.shape
    block_size = supernode_inverse.shape[1]
    row_blocks = row_count // block_size
    front_order = top_fronts.shape[1]
    front_blocks = front_order // block_size
    masked = coupling.reshape(row_blocks, block_size, col_count) * block_pattern[0].astype(
        jnp.bfloat16
    ).reshape(row_blocks, 1, 1)
    solved = jnp.einsum(
        "rbc,rab->cra", masked, supernode_inverse, preferred_element_type=jnp.float32
    ).reshape(col_count, row_count)
    live_rows = jnp.arange(row_count)[None, :] < subdomain_sizes[0]
    panel = jnp.where(live_rows, solved, 0.0).astype(jnp.bfloat16)
    gathered = lax.all_gather(panel, "front", axis=0, tiled=False)
    positions = jnp.arange(front_blocks)
    composite = block_maps[0, 0]
    for merge_level in range(1, levels):
        level_map = block_maps[merge_level, 0]
        composite = jnp.sum(
            jnp.where(composite[:, None] == positions[None, :], level_map[None, :], 0), axis=1
        )
    inverse = jnp.sum(
        jnp.where(composite[:, None] == positions[None, :], positions[:, None], 0), axis=0
    )
    source = lax.dynamic_index_in_dim(inverse, front_index, 0, keepdims=False)
    selected = lax.dynamic_index_in_dim(gathered, source, 0, keepdims=False)
    products = jnp.einsum("bck,dk->bcd", gathered, selected, preferred_element_type=jnp.float32)
    summed = -products[inverse]
    for merge_level in range(levels):
        summed = summed + from_partner(summed.astype(jnp.bfloat16), "leaf", merge_level).astype(
            summed.dtype
        )
    top_index = leaf_index // group_size
    top = lax.dynamic_index_in_dim(top_fronts, top_index, 0, keepdims=False)
    column = top + summed.reshape(front_order, col_count)
    block_row = leaf_index % group_size
    strips = lax.all_gather(column[:PIV], "front", axis=0, tiled=False)
    pivots = PIV // block_size
    corner = strips[:pivots].transpose(1, 0, 2).reshape(PIV, PIV)
    own_row = lax.dynamic_index_in_dim(strips, block_row, 0, keepdims=False)
    own = lax.dynamic_slice_in_dim(column, block_row * block_size, block_size)
    index = jnp.stack([block_row, front_index]).astype(jnp.int32)
    return finish(index, corner, own_row, column[:PIV], own)


def solution(mesh):
    return jax.shard_map(
        shards,
        mesh=mesh,
        in_specs=(
            P("leaf", "front"),
            P("leaf", None, "front"),
            P("leaf", None, None),
            P("leaf"),
            P(None, "leaf", None),
            P(None, None, "front"),
        ),
        out_specs=P("leaf", "front"),
        check_vma=False,
    )
```

time: 798 us -> 240 us (0.30)
  waiting for transfers between devices: 604 us -> 171 us
  other arithmetic: 101 us -> 7.35 us
  local copies, waits for them, and re-layouts: 27.6 us -> 7.99 us
  matrix products: 21.4 us -> 7.21 us
  Pallas kernels: 0 us -> 11.2 us
    psum x4 -> x0, waiting for transfers between devices: 467 us -> none  [spread(): return lax.psum(jnp.where(mine, value, jnp.zeros_like(value)), axis)]
    another operation x20 -> x1, other arithmetic: 91.4 us -> 0.61 us  [shards(): index = jnp.stack([block_row, front_index]).astype(jnp.int32)]
    all_gather x1 -> x2, waiting for transfers between devices: 68.6 us -> 102 us  [the longest x1 60.5 us: shards(): gathered = lax.all_gather(panel, 'front', axis=0, tiled=False)]
    dot_general x1 -> x0, local copies, waits for them, and re-layouts: 12.3 us -> none  [shards(): jnp.einsum('nk,nc->kc', gathered, selected, preferred_element_type=jnp.fl...]
    pallas_call x0 -> x1, Pallas kernels: none -> 11.2 us  [finish(): pl.pallas_call(finish_kernel, out_shape=jax.ShapeDtypeStruct((b, b), jnp....]
    dot_general x6 -> x2, matrix products: 18 us -> 7.21 us  [the longest x1 5.81 us: shards(): jnp.einsum('bck,dk->bcd', gathered, selected, preferred_element_type=jnp....]
    unnamed x9 -> x2, local copies, waits for them, and re-layouts: 9.78 us -> 0.34 us
  transfers between devices with their start and end apart: 9 -> 6, of which waited for: 9 -> 6; matrix products, arithmetic and copies ran while one was open for 0% -> 1% of each run, Pallas kernels for 0% -> 0%
where the time goes in v1:
time: 240 us; the launch traced here: 239 us
  waiting for transfers between devices  171 us (71%)
  starting transfers between devices  17.7 us (7%)
  between operations  16.1 us (7%)
  Pallas kernels  11.2 us (5%)
  local copies, waits for them, and re-layouts  7.99 us (3%)
  other arithmetic  7.35 us (3%)
  matrix products  7.21 us (3%)
    ppermute x4, waiting for transfers between devices, from_partner(): return lax.ppermute(value, axis, pairs)  69.1 us
    all_gather x1, waiting for transfers between devices, shards(): gathered = lax.all_gather(panel, 'front', axis=0, tiled=False)  60.5 us
    all_gather x1, waiting for transfers between devices, shards(): strips = lax.all_gather(column[:PIV], 'front', axis=0, tiled=False)  41.6 us
    ppermute x4, starting transfers between devices, from_partner(): return lax.ppermute(value, axis, pairs)  17.6 us
    pallas_call x1, Pallas kernels, finish(): pl.pallas_call(finish_kernel, out_shape=jax.ShapeDtypeStruct((b, b), jnp....  11.2 us
    dot_general x1, matrix products, shards(): jnp.einsum('bck,dk->bcd', gathered, selected, preferred_element_type=jnp....  5.81 us
  transfers between devices with their start and end apart: 6, of which 6 were waited for; matrix products, arithmetic and copies ran while one was open for 1% of the time, Pallas kernels for 0%

profile of v1, /device:TPU:7, one launch (start us, length us, event | category | flops | bytes accessed | tf_op | source)
XLA Modules:
  0.0 238.7 jit_solution(4330998224958751320)
XLA Ops:
  6.5 0.0 copy-start
  6.5 0.0 all-gather.4.cloned.1.call-start
  6.5 0.7 convert_bitcast_fusion
  7.3 0.3 copy-done
  7.6 1.4 fusion.4
  9.0 0.2 copy.11
  9.9 1.0 select_convert_fusion
  10.8 0.0 all-gather.4.cloned.1.call-update
  10.9 0.0 all-gather.6.cloned.1.call-start
  10.9 0.7 slice_bitcast_fusion.3
  11.6 0.2 select_reduce_fusion.3
  11.8 0.2 select_reduce_fusion.2
  12.0 0.2 select_reduce_fusion.1
  12.2 0.1 select_reduce_fusion
  12.3 0.6 dynamic_slice.20
  14.8 60.5 %all-gather.4.cloned.1.call-done = bf16[16,128,2048]{2,1,0:T(8,128)(2,1)} async-done(((bf16[1,128,2048]{2,1,0:T(8,128)(2,1)}), bf16[16,128,2048]{2,1,0:T(8,128)(2,1)}) %all-gather.4.cloned.1.call-update) | async-done | bytes 8388624 | tf_op jit(solution)/shard_map/all_gather | solution.py:140
  75.3 5.8 %fusion.1 = f32[16,128,128]{2,1,0:T(8,128)S(1)} fusion(bf16[16,128,2048]{2,1,0:T(8,128)(2,1)} %all-gather.4.cloned.1.call-done, s32[]{:T(128)S(6)} %select_n.74), kind=kOutput, calls=%fused_computation.10 | convolution fusion | flops 1073741824 | bytes 9961476 | tf_op jit(solution)/shard_map/bck,dk->bcd/dot_general | solution.py:153
  81.1 0.6 gather_fusion
  81.7 0.1 negate_convert_fusion
  81.9 3.1 %collective-permute-start = (bf16[16,128,128]{2,1,0:T(8,128)(2,1)S(1)}, bf16[16,128,128]{2,1,0:T(8,128)(2,1)S(1)}, u32[]{:S(2)}, u32[]{:S(2)}) collective-permute-start(bf16[16,128,128]{2,1,0:T(8,128)(2,1)S(1)} %negate_convert_fusion), channel_id=1, source_target_pairs={{0,16},{16,0},{32,48},{48,32},{64,80},{80,64},{96,112},{112,96},{1... | collective-permute-start | bytes 1572872 | tf_op jit(solution)/shard_map/ppermute | solution.py:118
  85.0 12.0 %collective-permute-done = bf16[16,128,128]{2,1,0:T(8,128)(2,1)S(1)} collective-permute-done((bf16[16,128,128]{2,1,0:T(8,128)(2,1)S(1)}, bf16[16,128,128]{2,1,0:T(8,128)(2,1)S(1)}, u32[]{:S(2)}, u32[]{:S(2)}) %collective-permute-start) | collective-permute-done | bytes 524320 | tf_op jit(solution)/shard_map/ppermute | solution.py:118
  97.0 0.2 fusion.10
  97.1 4.0 %collective-permute-start.1 = (bf16[16,128,128]{2,1,0:T(8,128)(2,1)S(1)}, bf16[16,128,128]{2,1,0:T(8,128)(2,1)S(1)}, u32[]{:S(2)}, u32[]{:S(2)}) collective-permute-start(bf16[16,128,128]{2,1,0:T(8,128)(2,1)S(1)} %fusion.10), channel_id=1, source_target_pairs={{0,32},{16,48},{32,0},{48,16},{64,96},{80,112},{96,64},{112,80},{1... | collective-permute-start | bytes 1572872 | tf_op jit(solution)/shard_map/ppermute | solution.py:118
  101.2 22.9 %collective-permute-done.1 = bf16[16,128,128]{2,1,0:T(8,128)(2,1)S(1)} collective-permute-done((bf16[16,128,128]{2,1,0:T(8,128)(2,1)S(1)}, bf16[16,128,128]{2,1,0:T(8,128)(2,1)S(1)}, u32[]{:S(2)}, u32[]{:S(2)}) %collective-permute-start.1) | collective-permute-done | bytes 524320 | tf_op jit(solution)/shard_map/ppermute | solution.py:118
  124.1 0.2 fusion
  124.3 8.0 %collective-permute-start.2 = (bf16[16,128,128]{2,1,0:T(8,128)(2,1)S(1)}, bf16[16,128,128]{2,1,0:T(8,128)(2,1)S(1)}, u32[]{:S(2)}, u32[]{:S(2)}) collective-permute-start(bf16[16,128,128]{2,1,0:T(8,128)(2,1)S(1)} %fusion), channel_id=1, source_target_pairs={{0,64},{16,80},{32,96},{48,112},{64,0},{80,16},{96,32},{112,48},{1... | collective-permute-start | bytes 1572872 | tf_op jit(solution)/shard_map/ppermute | solution.py:118
  132.3 22.7 %collective-permute-done.2 = bf16[16,128,128]{2,1,0:T(8,128)(2,1)S(1)} collective-permute-done((bf16[16,128,128]{2,1,0:T(8,128)(2,1)S(1)}, bf16[16,128,128]{2,1,0:T(8,128)(2,1)S(1)}, u32[]{:S(2)}, u32[]{:S(2)}) %collective-permute-start.2) | collective-permute-done | bytes 524320 | tf_op jit(solution)/shard_map/ppermute | solution.py:118
  154.9 1.1 fusion.6
  156.0 2.5 %collective-permute-start.3 = (bf16[16,128,128]{2,1,0:T(8,128)(2,1)}, bf16[16,128,128]{2,1,0:T(8,128)(2,1)}, u32[]{:S(2)}, u32[]{:S(2)}) collective-permute-start(bf16[16,128,128]{2,1,0:T(8,128)(2,1)} %fusion.6), channel_id=1, source_target_pairs={{0,128},{16,144},{32,160},{48,176},{64,192},{80,208},{96,224},{112... | collective-permute-start | bytes 1572872 | tf_op jit(solution)/shard_map/ppermute | solution.py:118
  158.5 11.6 %collective-permute-done.3 = bf16[16,128,128]{2,1,0:T(8,128)(2,1)} collective-permute-done((bf16[16,128,128]{2,1,0:T(8,128)(2,1)}, bf16[16,128,128]{2,1,0:T(8,128)(2,1)}, u32[]{:S(2)}, u32[]{:S(2)}) %collective-permute-start.3) | collective-permute-done | bytes 524320 | tf_op jit(solution)/shard_map/ppermute | solution.py:118
  170.1 1.4 convert_add_fusion
  171.5 1.4 bitcast_add_fusion
  172.9 0.7 slice.28.aj_ref
  173.7 0.0 all-gather.6.cloned.1.call-update
  173.7 0.6 pad_add_fusion.index_ref
  174.3 0.6 constant_dynamic-slice_fusion.aij_ref
  175.0 41.6 %all-gather.6.cloned.1.call-done = f32[8192,128]{1,0:T(8,128)} async-done(((f32[512,128]{1,0:T(8,128)}), f32[8192,128]{1,0:T(8,128)}) %all-gather.6.cloned.1.call-update) | async-done | bytes 4194320 | tf_op jit(solution)/shard_map/all_gather | solution.py:163
  216.6 1.3 slice.29
  217.9 1.1 copy.15
  219.0 1.7 dynamic-slice_bitcast_fusion.ai_ref
  220.7 11.2 %shard_map.64 = f32[128,128]{1,0:T(8,128)} custom-call(s32[2]{0:T(128)} %pad_add_fusion.index_ref, f32[512,512]{1,0:T(8,128)} %bitcast.43, f32[512,128]{1,0:T(8,128)} %dynamic-slice_bitcast_fusion.ai_ref, f32[512,128]{1,0:T(8,128)} %slice.28.aj_ref, f32[128,128]{1,0:T(8,128)} %constant_dynamic-slice_fusion.aij_ref), custom_call_target="tpu_custom_call" | custom-call | tf_op jit(solution)/shard_map/pallas_call | solution.py:104
  (3 shorter events, 0.0 us)
Async XLA Ops:
  6.5 1.1 copy-start
  6.5 68.8 %all-gather.4.cloned.1.call-start = ((), (), s32[]{:S(2)}) async-start(), calls=%async_computation | async-start | bytes 8912896 | tf_op jit(solution)/shard_map/all_gather | solution.py:140
  10.9 205.7 %all-gather.6.cloned.1.call-start = ((), (), s32[]{:S(2)}) async-start(), calls=%async_computation.1 | async-start | bytes 4456448 | tf_op jit(solution)/shard_map/all_gather | solution.py:163
  81.9 15.1 %collective-permute-start = (bf16[16,128,128]{2,1,0:T(8,128)(2,1)S(1)}, bf16[16,128,128]{2,1,0:T(8,128)(2,1)S(1)}, u32[]{:S(2)}, u32[]{:S(2)}) collective-permute-start(bf16[16,128,128]{2,1,0:T(8,128)(2,1)S(1)} %negate_convert_fusion), channel_id=1, source_target_pairs={{0,16},{16,0},{32,48},{48,32},{64,80},{80,64},{96,112},{112,96},{1... | collective-permute-start | bytes 1572872 | tf_op jit(solution)/shard_map/ppermute | solution.py:118
  97.1 26.9 %collective-permute-start.1 = (bf16[16,128,128]{2,1,0:T(8,128)(2,1)S(1)}, bf16[16,128,128]{2,1,0:T(8,128)(2,1)S(1)}, u32[]{:S(2)}, u32[]{:S(2)}) collective-permute-start(bf16[16,128,128]{2,1,0:T(8,128)(2,1)S(1)} %fusion.10), channel_id=1, source_target_pairs={{0,32},{16,48},{32,0},{48,16},{64,96},{80,112},{96,64},{112,80},{1... | collective-permute-start | bytes 1572872 | tf_op jit(solution)/shard_map/ppermute | solution.py:118
  124.3 30.7 %collective-permute-start.2 = (bf16[16,128,128]{2,1,0:T(8,128)(2,1)S(1)}, bf16[16,128,128]{2,1,0:T(8,128)(2,1)S(1)}, u32[]{:S(2)}, u32[]{:S(2)}) collective-permute-start(bf16[16,128,128]{2,1,0:T(8,128)(2,1)S(1)} %fusion), channel_id=1, source_target_pairs={{0,64},{16,80},{32,96},{48,112},{64,0},{80,16},{96,32},{112,48},{1... | collective-permute-start | bytes 1572872 | tf_op jit(solution)/shard_map/ppermute | solution.py:118
  156.0 14.1 %collective-permute-start.3 = (bf16[16,128,128]{2,1,0:T(8,128)(2,1)}, bf16[16,128,128]{2,1,0:T(8,128)(2,1)}, u32[]{:S(2)}, u32[]{:S(2)}) collective-permute-start(bf16[16,128,128]{2,1,0:T(8,128)(2,1)} %fusion.6), channel_id=1, source_target_pairs={{0,128},{16,144},{32,160},{48,176},{64,192},{80,208},{96,224},{112... | collective-permute-start | bytes 1572872 | tf_op jit(solution)/shard_map/ppermute | solution.py:118
Sparse Core Ops, SparseCore 0:
  11.0 64.2 all-gather.3
  173.8 42.7 all-gather.5

commit v2 on v1

--- a/solution.py
+++ b/solution.py
@@ -1,3 +1,5 @@
+import functools
+
 import jax
 import jax.numpy as jnp
 from jax import lax
@@ -25,9 +27,15 @@
     return mm(ah, bh, dims) + (mm(ah, bl, dims) + mm(al, bh, dims))
 
 
-def finish_kernel(index_ref, a_ref, ai_ref, aj_ref, aij_ref, out_ref, y_ref, w_ref):
+def finish_kernel(index_ref, corner_ref, ai_ref, aj_ref, aij_ref, out_ref, a_ref, y_ref, w_ref):
     n = a_ref.shape[0]
     b = ai_ref.shape[1]
+    for p in range(n // b):
+        for q in range(p + 1):
+            block = corner_ref[p, q]
+            a_ref[p * b : (p + 1) * b, q * b : (q + 1) * b] = block
+            if q < p:
+                a_ref[q * b : (q + 1) * b, p * b : (p + 1) * b] = block.T
     rows = lax.broadcasted_iota(jnp.int32, (n, n), 0)
     cols = lax.broadcasted_iota(jnp.int32, (n, n), 1)
     eye = (rows == cols).astype(jnp.float32)
@@ -97,25 +105,233 @@
     out_ref[...] = jnp.where(block_col >= pivots, right, left)
 
 
-def finish(index, a, ai, aj, aij):
-    n = a.shape[0]
-    b = ai.shape[1]
+def finish(index, corner, ai, aj, aij):
+    n, b = ai.shape
     vmem = pl.BlockSpec(memory_space=pltpu.VMEM)
     return pl.pallas_call(
         finish_kernel,
         out_shape=jax.ShapeDtypeStruct((b, b), jnp.float32),
         in_specs=[pl.BlockSpec(memory_space=pltpu.SMEM)] + [vmem] * 4,
         out_specs=vmem,
-        scratch_shapes=[pltpu.VMEM((n, n), jnp.float32), pltpu.VMEM((n, n), jnp.float32)],
-    )(index, a, ai, aj, aij)
+        scratch_shapes=[pltpu.VMEM((n, n), jnp.float32)] * 3,
+    )(index, corner, ai, aj, aij)
 
 PIV = 512
-
-
-def from_partner(value, axis, bit):
-    mask = 2**bit
-    pairs = [(source, source ^ mask) for source in range(lax.axis_size(axis))]
-    return lax.ppermute(value, axis, pairs)
+MESH = pl.DeviceIdType.MESH
+
+
+def leaf_sum_kernel(
+    group, chips, part_ref, top_ref, own_ref, corner_ref, row_ref, col_ref,
+    got_slice, got_block, piece, pieces,
+    slice_send, slice_recv, block_send, block_recv, piece_send, piece_recv,
+    plus_send, minus_send, twin_send, item_recv,
+):
+    blocks, b, _ = part_ref.shape
+    pivots = corner_ref.shape[0]
+    rows = piece.shape[0]
+    per_block = b // rows
+    leaf = lax.axis_index("leaf")
+    front = lax.axis_index("front")
+    base = leaf // group * group
+    me = leaf - base
+    z = front // 2
+    core = front % 2
+    twin = z * 2 + 1 - core
+    above = (z + 1) % chips * 2 + core
+    below = (z + chips - 1) % chips * 2 + core
+
+    def other(d):
+        return (me + d) % group
+
+    barrier = pltpu.get_barrier_semaphore()
+
+    def greet(d, carry):
+        pl.semaphore_signal(barrier, 1, device_id=(base + other(d), front), device_id_type=MESH)
+        return carry
+
+    lax.fori_loop(1, group, greet, 0)
+    for side in (twin, above, below):
+        pl.semaphore_signal(barrier, 1, device_id=(leaf, side), device_id_type=MESH)
+    pl.semaphore_wait(barrier, group - 1 + 3)
+
+    def slice_copy(to, src):
+        return pltpu.make_async_remote_copy(
+            part_ref.at[to // per_block, pl.ds(to % per_block * rows, rows), :],
+            got_slice.at[src], slice_send.at[to], slice_recv.at[src],
+            device_id=(base + to, front), device_id_type=MESH,
+        )
+
+    def block_copy(to, src):
+        return pltpu.make_async_remote_copy(
+            part_ref.at[to], got_block.at[src], block_send.at[to], block_recv.at[src],
+            device_id=(base + to, front), device_id_type=MESH,
+        )
+
+    def piece_copy(to, src):
+        return pltpu.make_async_remote_copy(
+            piece, pieces.at[src], piece_send.at[to], piece_recv.at[src],
+            device_id=(base + to, front), device_id_type=MESH,
+        )
+
+    inner = front >= pivots
+
+    def send_slice(d, carry):
+        slice_copy(other(d), me).start()
+        return carry
+
+    def send_block(d, carry):
+        to = other(d)
+
+        @pl.when(inner & (to >= pivots))
+        def _():
+            block_copy(to, me).start()
+
+        return carry
+
+    lax.fori_loop(1, group, send_slice, 0)
+    lax.fori_loop(1, group, send_block, 0)
+
+    def add_slice(d, total):
+        src = other(d)
+        slice_copy(src, src).wait_recv()
+        return total + got_slice[src].astype(jnp.float32)
+
+    mine = part_ref[me // per_block, pl.ds(pl.multiple_of(me % per_block * rows, rows), rows), :]
+    total = lax.fori_loop(1, group, add_slice, mine.astype(jnp.float32))
+    piece[...] = total.astype(jnp.bfloat16)
+    pieces[me] = total.astype(jnp.bfloat16)
+
+    def send_piece(d, carry):
+        piece_copy(other(d), me).start()
+        return carry
+
+    lax.fori_loop(1, group, send_piece, 0)
+
+    def wait_piece(d, carry):
+        src = other(d)
+        piece_copy(src, src).wait_recv()
+        return carry
+
+    lax.fori_loop(1, group, wait_piece, 0)
+    for p in range(pivots):
+        got = pieces[p * per_block : (p + 1) * per_block].astype(jnp.float32)
+        col_ref[p] = top_ref[p * b : (p + 1) * b, :] + got.reshape(b, b)
+
+    items = [(corner_ref, (p, q), q) for q in range(pivots) for p in range(q, pivots)]
+    items += [(row_ref, (p,), me) for p in range(pivots)]
+
+    def item_copy(n, sem, to):
+        ref, at, _ = items[n]
+        return pltpu.make_async_remote_copy(
+            ref.at[at], ref.at[at], sem.at[n], item_recv.at[n],
+            device_id=(leaf, to), device_id_type=MESH,
+        )
+
+    def roles(source):
+        lane = core == source % 2
+        far = (z + chips - source // 2) % chips
+        half = chips // 2
+        return lane, far, lane & (far < half), lane & ((far == 0) | (far > half + 1))
+
+    for n, (ref, at, source) in enumerate(items):
+        lane, far, plus, minus = roles(source)
+
+        @pl.when(lane & (far == 0))
+        def _():
+            ref[at] = col_ref[at[0]]
+
+        @pl.when(lane & (far != 0))
+        def _():
+            item_copy(n, twin_send, twin).wait_recv()
+
+        @pl.when(plus)
+        def _():
+            item_copy(n, plus_send, above).start()
+
+        @pl.when(minus)
+        def _():
+            item_copy(n, minus_send, below).start()
+
+        @pl.when(lane)
+        def _():
+            item_copy(n, twin_send, twin).start()
+
+    for n, (ref, at, source) in enumerate(items):
+        lane, far, plus, minus = roles(source)
+
+        @pl.when(jnp.logical_not(lane))
+        def _():
+            item_copy(n, twin_send, twin).wait_recv()
+
+    own_ref[...] = part_ref[me].astype(jnp.float32)
+
+    @pl.when(inner & (me >= pivots))
+    def _():
+        def add_block(d, carry):
+            src = other(d)
+            block_copy(src, src).wait_recv()
+            own_ref[...] = own_ref[...] + got_block[src].astype(jnp.float32)
+            return carry
+
+        lax.fori_loop(1, group, add_block, 0)
+
+    def drain(d, carry):
+        to = other(d)
+        slice_copy(to, me).wait_send()
+        piece_copy(to, me).wait_send()
+
+        @pl.when(inner & (to >= pivots))
+        def _():
+            block_copy(to, me).wait_send()
+
+        return carry
+
+    lax.fori_loop(1, group, drain, 0)
+    for n, (ref, at, source) in enumerate(items):
+        lane, far, plus, minus = roles(source)
+
+        @pl.when(plus)
+        def _():
+            item_copy(n, plus_send, above).wait_send()
+
+        @pl.when(minus)
+        def _():
+            item_copy(n, minus_send, below).wait_send()
+
+        @pl.when(lane)
+        def _():
+            item_copy(n, twin_send, twin).wait_send()
+
+
+def leaf_sum(part, top, group, chips):
+    blocks, b, _ = part.shape
+    pivots = PIV // b
+    rows = PIV // group
+    items = pivots * (pivots + 1) // 2 + pivots
+    vmem = pl.BlockSpec(memory_space=pltpu.VMEM)
+    dma = pltpu.SemaphoreType.DMA
+    f32 = jnp.float32
+    bf16 = jnp.bfloat16
+    return pl.pallas_call(
+        functools.partial(leaf_sum_kernel, group, chips),
+        out_shape=(
+            jax.ShapeDtypeStruct((b, b), f32),
+            jax.ShapeDtypeStruct((pivots, pivots, b, b), f32),
+            jax.ShapeDtypeStruct((pivots, b, b), f32),
+            jax.ShapeDtypeStruct((pivots, b, b), f32),
+        ),
+        in_specs=[vmem] * 2,
+        out_specs=[vmem] * 4,
+        scratch_shapes=[
+            pltpu.VMEM((group, rows, b), bf16),
+            pltpu.VMEM((group, b, b), bf16),
+            pltpu.VMEM((rows, b), bf16),
+            pltpu.VMEM((group, rows, b), bf16),
+        ]
+        + [dma((group,))] * 6
+        + [dma((items,))] * 4,
+        compiler_params=pltpu.CompilerParams(collective_id=1, has_side_effects=True),
+    )(part, top)
 
 
 def shards(coupling, block_pattern, supernode_inverse, subdomain_sizes, block_maps, top_fronts):
@@ -151,22 +367,16 @@
     source = lax.dynamic_index_in_dim(inverse, front_index, 0, keepdims=False)
     selected = lax.dynamic_index_in_dim(gathered, source, 0, keepdims=False)
     products = jnp.einsum("bck,dk->bcd", gathered, selected, preferred_element_type=jnp.float32)
-    summed = -products[inverse]
-    for merge_level in range(levels):
-        summed = summed + from_partner(summed.astype(jnp.bfloat16), "leaf", merge_level).astype(
-            summed.dtype
-        )
+    part = -products.astype(jnp.bfloat16)[inverse]
     top_index = leaf_index // group_size
     top = lax.dynamic_index_in_dim(top_fronts, top_index, 0, keepdims=False)
-    column = top + summed.reshape(front_order, col_count)
     block_row = leaf_index % group_size
-    strips = lax.all_gather(column[:PIV], "front", axis=0, tiled=False)
-    pivots = PIV // block_size
-    corner = strips[:pivots].transpose(1, 0, 2).reshape(PIV, PIV)
-    own_row = lax.dynamic_index_in_dim(strips, block_row, 0, keepdims=False)
-    own = lax.dynamic_slice_in_dim(column, block_row * block_size, block_size)
+    chips = lax.axis_size("front") // 2
+    own, corner, own_row, own_col = leaf_sum(part, top[:PIV], group_size, chips)
+    own = own + lax.dynamic_slice_in_dim(top, block_row * block_size, block_size)
     index = jnp.stack([block_row, front_index]).astype(jnp.int32)
-    return finish(index, corner, own_row, column[:PIV], own)
+    flat = (PIV, block_size)
+    return finish(index, corner, own_row.reshape(flat), own_col.reshape(flat), own)
 
 
 def solution(mesh):

time: 240 us -> 161 us (0.67)
  waiting for transfers between devices: 171 us -> 58.2 us
  Pallas kernels: 11.2 us -> 69.3 us
  starting transfers between devices: 17.7 us -> 0.01 us
  local copies, waits for them, and re-layouts: 7.99 us -> 4.25 us
    ppermute x4 -> x0, waiting for transfers between devices: 69.1 us -> none  [from_partner(): return lax.ppermute(value, axis, pairs)]
    pallas_call x0 -> x1, Pallas kernels: none -> 58 us  [leaf_sum(): pl.pallas_call(functools.partial(leaf_sum_kernel, group, chips), out_shap...]
    all_gather x1 -> x0, waiting for transfers between devices: 41.6 us -> none  [shards(): strips = lax.all_gather(column[:PIV], 'front', axis=0, tiled=False)]
    ppermute x4 -> x0, starting transfers between devices: 17.6 us -> none  [from_partner(): return lax.ppermute(value, axis, pairs)]
  transfers between devices with their start and end apart: 6 -> 1, of which waited for: 6 -> 1; matrix products, arithmetic and copies ran while one was open for 1% -> 3% of each run, Pallas kernels for 0% -> 0%
where the time goes in v2:
time: 161 us; the launch traced here: 160 us
  Pallas kernels  69.3 us (43%)
  waiting for transfers between devices  58.2 us (36%)
  between operations  16 us (10%)
  matrix products  7.18 us (4%)
  other arithmetic  5.44 us (3%)
  local copies, waits for them, and re-layouts  4.25 us (3%)
    all_gather x1, waiting for transfers between devices, shards(): gathered = lax.all_gather(panel, 'front', axis=0, tiled=False)  58.2 us
    pallas_call x1, Pallas kernels, leaf_sum(): pl.pallas_call(functools.partial(leaf_sum_kernel, group, chips), out_shap...  58 us
    pallas_call x1, Pallas kernels, finish(): pl.pallas_call(finish_kernel, out_shape=jax.ShapeDtypeStruct((b, b), jnp....  11.3 us
    dot_general x1, matrix products, shards(): jnp.einsum('bck,dk->bcd', gathered, selected, preferred_element_type=jnp....  5.78 us
  transfers between devices with their start and end apart: 1, of which 1 were waited for; matrix products, arithmetic and copies ran while one was open for 3% of the time, Pallas kernels for 0%

profile of v2, /device:TPU:7, one launch (start us, length us, event | category | flops | bytes accessed | tf_op | source)
XLA Modules:
  0.0 160.4 jit_solution(4039858279525537715)
XLA Ops:
  6.5 0.0 copy-start
  6.5 0.0 all-gather.2.cloned.1.call-start
  6.5 0.7 convert_bitcast_fusion
  7.3 0.3 copy-done
  7.6 1.4 fusion.2
  9.0 0.2 copy.9
  9.9 1.0 select_convert_fusion
  10.8 0.0 all-gather.2.cloned.1.call-update
  10.9 0.7 slice_bitcast_fusion.3
  11.6 0.2 select_reduce_fusion.3
  11.8 0.2 select_reduce_fusion.2
  12.0 0.2 select_reduce_fusion.1
  12.1 0.1 select_reduce_fusion
  12.2 0.6 dynamic_slice.17
  14.8 0.6 pad_add_fusion.index_ref
  15.4 1.7 %dynamic-slice_bitcast_fusion.top_ref = f32[512,128]{1,0:T(8,128)} fusion(f32[2,2048,128]{2,1,0:T(8,128)} %param.11, s32[]{:T(128)S(6)} %select_n.75), kind=kLoop, calls=%fused_computation.7 | loop fusion | bytes 524292 | tf_op jit(solution)/shard_map/slice | solution.py:375
  17.1 58.2 %all-gather.2.cloned.1.call-done = bf16[16,128,2048]{2,1,0:T(8,128)(2,1)} async-done(((bf16[1,128,2048]{2,1,0:T(8,128)(2,1)}), bf16[16,128,2048]{2,1,0:T(8,128)(2,1)}) %all-gather.2.cloned.1.call-update) | async-done | bytes 8388624 | tf_op jit(solution)/shard_map/all_gather | solution.py:356
  75.3 5.8 %convolution_convert_fusion = bf16[16,128,128]{2,1,0:T(8,128)(2,1)S(1)} fusion(bf16[16,128,2048]{2,1,0:T(8,128)(2,1)} %all-gather.2.cloned.1.call-done, s32[]{:T(128)S(6)} %select_n.72), kind=kOutput, calls=%fused_computation.1 | convolution fusion | flops 1074003968 | bytes 9437188 | tf_op jit(solution)/shard_map/bck,dk->bcd/dot_general | solution.py:369
  81.1 0.6 gather_fusion
  81.8 1.0 neg.3.part_ref
  82.7 58.0 %shard_map.64 = (f32[128,128]{1,0:T(8,128)}, f32[4,4,128,128]{3,2,1,0:T(8,128)}, f32[4,128,128]{2,1,0:T(8,128)}, f32[4,128,128]{2,1,0:T(8,128)}) custom-call(bf16[16,128,128]{2,1,0:T(8,128)(2,1)} %neg.3.part_ref, f32[512,128]{1,0:T(8,128)} %dynamic-slice_bitcast_fusion.top_ref), custom_call_target="tpu_custom_call" | custom-call | tf_op jit(solution)/shard_map/pallas_call | solution.py:315
  140.7 1.6 bitcast_add_fusion.aij_ref
  142.3 11.3 %shard_map.65 = f32[128,128]{1,0:T(8,128)} custom-call(s32[2]{0:T(128)} %pad_add_fusion.index_ref, f32[4,4,128,128]{3,2,1,0:T(8,128)} %get-tuple-element.9.corner_ref, f32[512,128]{1,0:T(8,128)} %bitcast.37, f32[512,128]{1,0:T(8,128)} %bitcast.38, f32[128,128]{1,0:T(8,128)} %bitcast_add_fusion.aij_ref), custom_call_target="tpu_custom_call" | custom-call | tf_op jit(solution)/shard_map/pallas_call | solution.py:111
  (3 shorter events, 0.0 us)
Async XLA Ops:
  6.5 1.1 copy-start
  6.5 68.8 %all-gather.2.cloned.1.call-start = ((), (), s32[]{:S(2)}) async-start(), calls=%async_computation | async-start | bytes 8912896 | tf_op jit(solution)/shard_map/all_gather | solution.py:356
Sparse Core Ops, SparseCore 0:
  11.0 64.2 all-gather.1

commit v3 on v2

--- a/solution.py
+++ b/solution.py
@@ -27,7 +27,7 @@
     return mm(ah, bh, dims) + (mm(ah, bl, dims) + mm(al, bh, dims))
 
 
-def finish_kernel(index_ref, corner_ref, ai_ref, aj_ref, aij_ref, out_ref, a_ref, y_ref, w_ref):
+def finish_kernel(group, corner_ref, ai_ref, aj_ref, aij_ref, out_ref, a_ref, y_ref, w_ref):
     n = a_ref.shape[0]
     b = ai_ref.shape[1]
     for p in range(n // b):
@@ -89,8 +89,8 @@
 
         lax.fori_loop(0, n, eliminate, 0)
 
-    block_row = index_ref[0]
-    block_col = index_ref[1]
+    block_row = lax.axis_index("leaf") % group
+    block_col = lax.axis_index("front")
     pivots = n // b
     y = y_ref[...]
     xi = mm3(y, ai_ref[...], NN)
@@ -105,24 +105,27 @@
     out_ref[...] = jnp.where(block_col >= pivots, right, left)
 
 
-def finish(index, corner, ai, aj, aij):
+def finish(group, corner, ai, aj, aij):
     n, b = ai.shape
     vmem = pl.BlockSpec(memory_space=pltpu.VMEM)
     return pl.pallas_call(
-        finish_kernel,
+        functools.partial(finish_kernel, group),
         out_shape=jax.ShapeDtypeStruct((b, b), jnp.float32),
-        in_specs=[pl.BlockSpec(memory_space=pltpu.SMEM)] + [vmem] * 4,
+        in_specs=[vmem] * 4,
         out_specs=vmem,
         scratch_shapes=[pltpu.VMEM((n, n), jnp.float32)] * 3,
-    )(index, corner, ai, aj, aij)
+    )(corner, ai, aj, aij)
 
 PIV = 512
 MESH = pl.DeviceIdType.MESH
 
 
-def leaf_sum_kernel(
-    group, chips, part_ref, top_ref, own_ref, corner_ref, row_ref, col_ref,
+def assemble_kernel(
+    group, chips, coupling_ref, factor_ref, tops_ref, pattern_ref, size_ref, map_ref,
+    own_ref, corner_ref, row_ref, col_ref,
+    bufs, acc, part_ref, top_ref, block_ref,
     got_slice, got_block, piece, pieces,
+    chunk_recv, chunk_plus, chunk_minus, chunk_twin, top_sem,
     slice_send, slice_recv, block_send, block_recv, piece_send, piece_recv,
     plus_send, minus_send, twin_send, item_recv,
 ):
@@ -143,6 +146,15 @@
     def other(d):
         return (me + d) % group
 
+    top_copy = pltpu.make_async_copy(
+        tops_ref.at[leaf // group, pl.ds(0, pivots * b), :], top_ref, top_sem.at[0]
+    )
+    own_copy = pltpu.make_async_copy(
+        tops_ref.at[leaf // group, pl.ds(pl.multiple_of(me * b, b), b), :], block_ref, top_sem.at[1]
+    )
+    top_copy.start()
+    own_copy.start()
+
     barrier = pltpu.get_barrier_semaphore()
 
     def greet(d, carry):
@@ -152,7 +164,113 @@
     lax.fori_loop(1, group, greet, 0)
     for side in (twin, above, below):
         pl.semaphore_signal(barrier, 1, device_id=(leaf, side), device_id_type=MESH)
+
+    parts = len(bufs)
+    supers = factor_ref.shape[0] // parts
+    half = chips // 2
+    row_id = lax.broadcasted_iota(jnp.int32, (b, b), 0)
+
+    def solve(k):
+        for r in range(supers):
+            n = k * supers + r
+            solved = mm(factor_ref[n], coupling_ref[n * b : (n + 1) * b, :], NN)
+            live = jnp.where(row_id + n * b < size_ref[0], pattern_ref[0, n, 0], 0)
+            kept = jnp.where(live > 0, solved, 0.0)
+            bufs[k][front, :, r * b : (r + 1) * b] = kept.T.astype(jnp.bfloat16)
+
+    def chunk_copy(k, block, sem, to):
+        return pltpu.make_async_remote_copy(
+            bufs[k].at[block], bufs[k].at[block], sem.at[k, block], chunk_recv.at[k, block],
+            device_id=(leaf, to), device_id_type=MESH,
+        )
+
+    def block_at(d):
+        return (z + d + chips) % chips * 2 + core
+
+    def reach(k):
+        return (half, half - 1) if k % 2 == 0 else (half - 1, half)
+
+    def launch(k):
+        chunk_copy(k, front, chunk_plus, above).start()
+        chunk_copy(k, front, chunk_minus, below).start()
+        chunk_copy(k, front, chunk_twin, twin).start()
+
+    def relay(k, d):
+        up, down = reach(k)
+        if d <= up:
+            block = block_at(-d)
+            chunk_copy(k, block, chunk_plus, above).wait_recv()
+            if d < up:
+                chunk_copy(k, block, chunk_plus, above).start()
+            chunk_copy(k, block, chunk_twin, twin).start()
+        if d <= down:
+            block = block_at(d)
+            chunk_copy(k, block, chunk_minus, below).wait_recv()
+            if d < down:
+                chunk_copy(k, block, chunk_minus, below).start()
+            chunk_copy(k, block, chunk_twin, twin).start()
+
+    def twins(k):
+        def one(n, carry):
+            chunk_copy(k, n * 2 + 1 - core, chunk_twin, twin).wait_recv()
+            return carry
+
+        lax.fori_loop(0, chips, one, 0)
+
+    places = []
+    for n in range(blocks):
+        place = n
+        for level in range(map_ref.shape[0]):
+            place = map_ref[level, 0, place]
+        places.append(place)
+
+    def source(at):
+        found = [jnp.where(places[n] == at, n, 0) for n in range(blocks)]
+        return functools.reduce(jnp.maximum, found)
+
+    def gram(k):
+        picked = bufs[k][source(front)]
+
+        def one(n, carry):
+            two = bufs[k][pl.ds(n * 2, 2)].reshape(2 * b, picked.shape[1])
+            add = mm(two, picked, NT).reshape(2, b, b)
+            if k == 0:
+                acc[pl.ds(n * 2, 2)] = add
+            else:
+                acc[pl.ds(n * 2, 2)] = acc[pl.ds(n * 2, 2)] + add
+            return carry
+
+        lax.fori_loop(0, blocks // 2, one, 0, unroll=True)
+
+    solve(0)
     pl.semaphore_wait(barrier, group - 1 + 3)
+    launch(0)
+    solve(1)
+    launch(1)
+    for k in range(2, parts):
+        solve(k)
+    for d in range(1, half + 1):
+        for k in (0, 1):
+            relay(k, d)
+            if d == half - 1:
+                launch(k + 2)
+    twins(0)
+    relay(2, 1)
+    relay(3, 1)
+    gram(0)
+    relay(2, 2)
+    relay(3, 2)
+    twins(1)
+    gram(1)
+    for d in range(3, half + 1):
+        relay(2, d)
+        relay(3, d)
+    twins(2)
+    gram(2)
+    twins(3)
+    gram(3)
+    for at in range(blocks):
+        part_ref[at] = -acc[source(at)].astype(jnp.bfloat16)
 
     def slice_copy(to, src):
         return pltpu.make_async_remote_copy(
@@ -213,6 +331,8 @@
         return carry
 
     lax.fori_loop(1, group, wait_piece, 0)
+    top_copy.wait()
+    own_copy.wait()
     for p in range(pivots):
         got = pieces[p * per_block : (p + 1) * per_block].astype(jnp.float32)
         col_ref[p] = top_ref[p * b : (p + 1) * b, :] + got.reshape(b, b)
@@ -263,7 +383,7 @@
         def _():
             item_copy(n, twin_send, twin).wait_recv()
 
-    own_ref[...] = part_ref[me].astype(jnp.float32)
+    own_ref[...] = block_ref[...] + part_ref[me].astype(jnp.float32)
 
     @pl.when(inner & (me >= pivots))
     def _():
@@ -302,81 +422,71 @@
         def _():
             item_copy(n, twin_send, twin).wait_send()
 
-
-def leaf_sum(part, top, group, chips):
-    blocks, b, _ = part.shape
+    for k in range(parts):
+        up, down = reach(k)
+        for d in range(half + 1):
+            if d < up:
+                chunk_copy(k, block_at(-d), chunk_plus, above).wait_send()
+            if d < down:
+                chunk_copy(k, block_at(d), chunk_minus, below).wait_send()
+
+        def sent(n, carry):
+            chunk_copy(k, n * 2 + core, chunk_twin, twin).wait_send()
+            return carry
+
+        lax.fori_loop(0, chips, sent, 0)
+
+
+def assemble(group, chips, coupling, factors, tops, pattern, sizes, maps):
+    b = coupling.shape[1]
+    blocks = tops.shape[1] // b
     pivots = PIV // b
     rows = PIV // group
     items = pivots * (pivots + 1) // 2 + pivots
+    parts = 4
     vmem = pl.BlockSpec(memory_space=pltpu.VMEM)
+    smem = pl.BlockSpec(memory_space=pltpu.SMEM)
     dma = pltpu.SemaphoreType.DMA
     f32 = jnp.float32
     bf16 = jnp.bfloat16
     return pl.pallas_call(
-        functools.partial(leaf_sum_kernel, group, chips),
+        functools.partial(assemble_kernel, group, chips),
         out_shape=(
             jax.ShapeDtypeStruct((b, b), f32),
             jax.ShapeDtypeStruct((pivots, pivots, b, b), f32),
             jax.ShapeDtypeStruct((pivots, b, b), f32),
             jax.ShapeDtypeStruct((pivots, b, b), f32),
         ),
-        in_specs=[vmem] * 2,
+        in_specs=[vmem] * 2 + [pl.BlockSpec(memory_space=pl.ANY)] + [smem] * 3,
         out_specs=[vmem] * 4,
         scratch_shapes=[
+            [pltpu.VMEM((blocks, b, coupling.shape[0] // parts), bf16)] * parts,
+            pltpu.VMEM((blocks, b, b), f32),
+            pltpu.VMEM((blocks, b, b), bf16),
+            pltpu.VMEM((PIV, b), f32),
+            pltpu.VMEM((b, b), f32),
             pltpu.VMEM((group, rows, b), bf16),
             pltpu.VMEM((group, b, b), bf16),
             pltpu.VMEM((rows, b), bf16),
             pltpu.VMEM((group, rows, b), bf16),
         ]
+        + [dma((parts, blocks))] * 4
+        + [dma((2,))]
         + [dma((group,))] * 6
         + [dma((items,))] * 4,
         compiler_params=pltpu.CompilerParams(collective_id=1, has_side_effects=True),
-    )(part, top)
+    )(coupling, factors, tops, pattern, sizes, maps)
 
 
 def shards(coupling, block_pattern, supernode_inverse, subdomain_sizes, block_maps, top_fronts):
-    leaf_count = lax.axis_size("leaf")
-    leaf_index = lax.axis_index("leaf")
-    front_index = lax.axis_index("front")
-    levels = block_maps.shape[0]
-    group_size = leaf_count // top_fronts.shape[0]
-    row_count, col_count = coupling.shape
-    block_size = supernode_inverse.shape[1]
-    row_blocks = row_count // block_size
-    front_order = top_fronts.shape[1]
-    front_blocks = front_order // block_size
-    masked = coupling.reshape(row_blocks, block_size, col_count) * block_pattern[0].astype(
-        jnp.bfloat16
-    ).reshape(row_blocks, 1, 1)
-    solved = jnp.einsum(
-        "rbc,rab->cra", masked, supernode_inverse, preferred_element_type=jnp.float32
-    ).reshape(col_count, row_count)
-    live_rows = jnp.arange(row_count)[None, :] < subdomain_sizes[0]
-    panel = jnp.where(live_rows, solved, 0.0).astype(jnp.bfloat16)
-    gathered = lax.all_gather(panel, "front", axis=0, tiled=False)
-    positions = jnp.arange(front_blocks)
-    composite = block_maps[0, 0]
-    for merge_level in range(1, levels):
-        level_map = block_maps[merge_level, 0]
-        composite = jnp.sum(
-            jnp.where(composite[:, None] == positions[None, :], level_map[None, :], 0), axis=1
-        )
-    inverse = jnp.sum(
-        jnp.where(composite[:, None] == positions[None, :], positions[:, None], 0), axis=0
+    group = lax.axis_size("leaf") // top_fronts.shape[0]
+    chips = lax.axis_size("front") // 2
+    own, corner, own_row, own_col = assemble(
+        group, chips, coupling, supernode_inverse, top_fronts,
+        block_pattern, subdomain_sizes, block_maps,
     )
-    source = lax.dynamic_index_in_dim(inverse, front_index, 0, keepdims=False)
-    selected = lax.dynamic_index_in_dim(gathered, source, 0, keepdims=False)
-    products = jnp.einsum("bck,dk->bcd", gathered, selected, preferred_element_type=jnp.float32)
-    part = -products.astype(jnp.bfloat16)[inverse]
-    top_index = leaf_index // group_size
-    top = lax.dynamic_index_in_dim(top_fronts, top_index, 0, keepdims=False)
-    block_row = leaf_index % group_size
-    chips = lax.axis_size("front") // 2
-    own, corner, own_row, own_col = leaf_sum(part, top[:PIV], group_size, chips)
-    own = own + lax.dynamic_slice_in_dim(top, block_row * block_size, block_size)
-    index = jnp.stack([block_row, front_index]).astype(jnp.int32)
-    flat = (PIV, block_size)
-    return finish(index, corner, own_row.reshape(flat), own_col.reshape(flat), own)
+    flat = (PIV, coupling.shape[1])
+    return finish(group, corner, own_row.reshape(flat), own_col.reshape(flat), own)
 
 
 def solution(mesh):

time: 161 us -> 131 us (0.81)
  Pallas kernels: 69.3 us -> 129 us
  waiting for transfers between devices: 58.2 us -> 0 us
  between operations: 16 us -> 0.66 us
  matrix products: 7.18 us -> 0 us
  other arithmetic: 5.44 us -> 0 us
  local copies, waits for them, and re-layouts: 4.25 us -> 1.33 us
    pallas_call x2, Pallas kernels: 69.3 us -> 129 us  [the longest x1 117 us: assemble(): pl.pallas_call(functools.partial(assemble_kernel, group, chips), out_shap...]
    all_gather x1 -> x0, waiting for transfers between devices: 58.2 us -> none  [shards(): gathered = lax.all_gather(panel, 'front', axis=0, tiled=False)]
    dot_general x2 -> x0, matrix products: 7.18 us -> none  [the longest x1 5.78 us: shards(): jnp.einsum('bck,dk->bcd', gathered, selected, preferred_element_type=jnp....]
    slice x1 -> x0, local copies, waits for them, and re-layouts: 1.7 us -> none  [shards(): own, corner, own_row, own_col = leaf_sum(part, top[:PIV], group_size, chips)]
    convert_element_type x2 -> x0, other arithmetic: 1.67 us -> none  [the longest x1 0.95 us: shards(): panel = jnp.where(live_rows, solved, 0.0).astype(jnp.bfloat16)]
  transfers between devices with their start and end apart: 1 -> 0, of which waited for: 1 -> 0; matrix products, arithmetic and copies ran while one was open for 3% -> 0% of each run, Pallas kernels for 0% -> 0%
where the time goes in v3:
time: 131 us
  Pallas kernels  129 us (98%)
  local copies, waits for them, and re-layouts  1.33 us (1%)
    pallas_call x1, Pallas kernels, assemble(): pl.pallas_call(functools.partial(assemble_kernel, group, chips), out_shap...  117 us
    pallas_call x1, Pallas kernels, finish(): pl.pallas_call(functools.partial(finish_kernel, group), out_shape=jax.Sha...  11.3 us

profile of v3, /device:TPU:7, one launch (start us, length us, event | category | flops | bytes accessed | tf_op | source)
XLA Modules:
  0.0 130.7 jit_solution(12244342762223714481)
XLA Ops:
  0.7 1.3 %copy.7.pattern_ref = s32[1,16,1]{2,1,0:T(8,128)} copy(s32[1,16,1]{1,2,0:T(1,128)} %param.7) | data formatting | bytes 128 | tf_op args[1]
  2.0 117.4 %shard_map.64 = (f32[128,128]{1,0:T(8,128)}, f32[4,4,128,128]{3,2,1,0:T(8,128)}, f32[4,128,128]{2,1,0:T(8,128)}, f32[4,128,128]{2,1,0:T(8,128)}) custom-call(bf16[2048,128]{1,0:T(8,128)(2,1)} %coupling_ref.1, bf16[16,128,128]{2,1,0:T(8,128)(2,1)} %factor_ref.1, f32[2,2048,128]{2,1,0:T(8,128)} %tops_ref.1, s32[1,16,1]{2,1,0:T(8,128)} %copy.7.pattern_ref, ...), custom_call_target="tpu_custom_call" | custom-call | tf_op jit(solution)/shard_map/pallas_call | solution.py:452
  119.4 11.3 %shard_map.65 = f32[128,128]{1,0:T(8,128)} custom-call(f32[4,4,128,128]{3,2,1,0:T(8,128)} %get-tuple-element.9.corner_ref, f32[512,128]{1,0:T(8,128)} %bitcast.2, f32[512,128]{1,0:T(8,128)} %bitcast.3, f32[128,128]{1,0:T(8,128)} %get-tuple-element.12.aij_ref), custom_call_target="tpu_custom_call" | custom-call | tf_op jit(solution)/shard_map/pallas_call | solution.py:111

commit v4 on v3

--- a/solution.py
+++ b/solution.py
@@ -307,7 +307,6 @@
         return carry
 
     lax.fori_loop(1, group, send_slice, 0)
-    lax.fori_loop(1, group, send_block, 0)
 
     def add_slice(d, total):
         src = other(d)
@@ -324,6 +323,7 @@
         return carry
 
     lax.fori_loop(1, group, send_piece, 0)
+    lax.fori_loop(1, group, send_block, 0)
 
     def wait_piece(d, carry):
         src = other(d)
@@ -359,22 +359,31 @@
         @pl.when(lane & (far == 0))
         def _():
             ref[at] = col_ref[at[0]]
-
-        @pl.when(lane & (far != 0))
-        def _():
-            item_copy(n, twin_send, twin).wait_recv()
-
-        @pl.when(plus)
-        def _():
             item_copy(n, plus_send, above).start()
-
-        @pl.when(minus)
-        def _():
             item_copy(n, minus_send, below).start()
-
-        @pl.when(lane)
-        def _():
             item_copy(n, twin_send, twin).start()
+
+    def hop(t, carry):
+        for n, (ref, at, source) in enumerate(items):
+            lane, far, plus, minus = roles(source)
+
+            @pl.when(lane & (jnp.minimum(far, chips - far) == t))
+            def _():
+                item_copy(n, twin_send, twin).wait_recv()
+
+                @pl.when(plus)
+                def _():
+                    item_copy(n, plus_send, above).start()
+
+                @pl.when(minus)
+                def _():
+                    item_copy(n, minus_send, below).start()
+
+                item_copy(n, twin_send, twin).start()
+
+        return carry
+
+    lax.fori_loop(1, chips // 2 + 1, hop, 0)
 
     for n, (ref, at, source) in enumerate(items):
         lane, far, plus, minus = roles(source)

time: 131 us -> 116 us (0.89)
  Pallas kernels: 129 us -> 113 us
    pallas_call x1, Pallas kernels: 117 us -> 102 us  [assemble(): pl.pallas_call(functools.partial(assemble_kernel, group, chips), out_shap...]
where the time goes in v4:
time: 116 us; the launch traced here: 115 us
  Pallas kernels  113 us (97%)
  local copies, waits for them, and re-layouts  1.33 us (1%)
    pallas_call x1, Pallas kernels, assemble(): pl.pallas_call(functools.partial(assemble_kernel, group, chips), out_shap...  102 us
    pallas_call x1, Pallas kernels, finish(): pl.pallas_call(functools.partial(finish_kernel, group), out_shape=jax.Sha...  11.3 us

profile of v4, /device:TPU:7, one launch (start us, length us, event | category | flops | bytes accessed | tf_op | source)
XLA Modules:
  0.0 115.0 jit_solution(3043979383928350022)
XLA Ops:
  0.7 1.3 %copy.7.pattern_ref = s32[1,16,1]{2,1,0:T(8,128)} copy(s32[1,16,1]{1,2,0:T(1,128)} %param.7) | data formatting | bytes 128 | tf_op args[1]
  2.0 101.7 %shard_map.64 = (f32[128,128]{1,0:T(8,128)}, f32[4,4,128,128]{3,2,1,0:T(8,128)}, f32[4,128,128]{2,1,0:T(8,128)}, f32[4,128,128]{2,1,0:T(8,128)}) custom-call(bf16[2048,128]{1,0:T(8,128)(2,1)} %coupling_ref.1, bf16[16,128,128]{2,1,0:T(8,128)(2,1)} %factor_ref.1, f32[2,2048,128]{2,1,0:T(8,128)} %tops_ref.1, s32[1,16,1]{2,1,0:T(8,128)} %copy.7.pattern_ref, ...), custom_call_target="tpu_custom_call" | custom-call | tf_op jit(solution)/shard_map/pallas_call | solution.py:461
  103.7 11.3 %shard_map.65 = f32[128,128]{1,0:T(8,128)} custom-call(f32[4,4,128,128]{3,2,1,0:T(8,128)} %get-tuple-element.9.corner_ref, f32[512,128]{1,0:T(8,128)} %bitcast.2, f32[512,128]{1,0:T(8,128)} %bitcast.3, f32[128,128]{1,0:T(8,128)} %get-tuple-element.12.aij_ref), custom_call_target="tpu_custom_call" | custom-call | tf_op jit(solution)/shard_map/pallas_call | solution.py:111

commit v5 on v3

--- a/solution.py
+++ b/solution.py
@@ -27,8 +27,9 @@
     return mm(ah, bh, dims) + (mm(ah, bl, dims) + mm(al, bh, dims))
 
 
-def finish_kernel(group, corner_ref, ai_ref, aj_ref, aij_ref, out_ref, a_ref, y_ref, w_ref):
+def finish_kernel(group, corner_ref, ai_ref, aj_ref, aij_ref, out_ref, a_ref, y_ref, w_ref, ah_ref, al_ref):
     n = a_ref.shape[0]
+    h = n // 2
     b = ai_ref.shape[1]
     for p in range(n // b):
         for q in range(p + 1):
@@ -36,42 +37,73 @@
             a_ref[p * b : (p + 1) * b, q * b : (q + 1) * b] = block
             if q < p:
                 a_ref[q * b : (q + 1) * b, p * b : (p + 1) * b] = block.T
-    rows = lax.broadcasted_iota(jnp.int32, (n, n), 0)
-    cols = lax.broadcasted_iota(jnp.int32, (n, n), 1)
+    rows = lax.broadcasted_iota(jnp.int32, (h, h), 0)
+    cols = lax.broadcasted_iota(jnp.int32, (h, h), 1)
     eye = (rows == cols).astype(jnp.float32)
     weight = jnp.where(rows > cols, 1.0, jnp.where(rows == cols, 0.5, 0.0))
-    diag = jnp.sum(a_ref[...] * eye, axis=0, keepdims=True)
-    y_ref[...] = eye * lax.rsqrt(diag)
+    for at in (0, h):
+        diag = jnp.sum(a_ref[at : at + h, at : at + h] * eye, axis=0, keepdims=True)
+        y_ref[at : at + h, at : at + h] = eye * lax.rsqrt(diag)
+        y_ref[at : at + h, h - at : n - at] = jnp.zeros((h, h), jnp.float32)
+    ah, al = halves(a_ref[...])
+    ah_ref[...] = ah
+    al_ref[...] = al
 
     def rough(_, carry):
-        ab = a_ref[...].astype(jnp.bfloat16)
-        yb = y_ref[...].astype(jnp.bfloat16)
-        g = mm(ab, yb, NT).astype(jnp.bfloat16)
-        e = (mm(yb, g, NN) - eye) * weight
-        y_ref[...] = y_ref[...] - mm(e.astype(jnp.bfloat16), yb, NN)
+        ab = ah_ref[...]
+        y1 = y_ref[:h, :h].astype(jnp.bfloat16)
+        y2 = y_ref[h:, :].astype(jnp.bfloat16)
+        g1 = mm(ab[:, :h], y1, NT).astype(jnp.bfloat16)
+        g2 = mm(ab, y2, NT).astype(jnp.bfloat16)
+        e1 = (mm(y1, g1[:h], NN) - eye) * weight
+        e21 = mm(y2, g1, NN)
+        e22 = (mm(y2, g2, NN) - eye) * weight
+        e1 = e1.astype(jnp.bfloat16)
+        e21 = e21.astype(jnp.bfloat16)
+        e22 = e22.astype(jnp.bfloat16)
+        y_ref[:h, :h] = y_ref[:h, :h] - mm(e1, y1, NN)
+        y_ref[h:, :h] = y_ref[h:, :h] - mm(e21, y1, NN) - mm(e22, y2[:, :h], NN)
+        y_ref[h:, h:] = y_ref[h:, h:] - mm(e22, y2[:, h:], NN)
         return carry
 
     lax.fori_loop(0, 2, rough, 0)
+
+    def pair(x, y, dims):
+        (xh, xl), (yh, yl) = x, y
+        return mm(xh, yh, dims) + (mm(xh, yl, dims) + mm(xl, yh, dims))
 
     def fine(carry):
         step, _ = carry
-        y = y_ref[...]
-        e = (mm3(y, mm3(a_ref[...], y, NT), NN) - eye) * weight
-        y_ref[...] = y - mm3(e, y, NN)
-        return step + 1, jnp.max(jnp.abs(e))
+        y1 = halves(y_ref[:h, :h])
+        y2 = halves(y_ref[h:, :])
+        y21 = (y2[0][:, :h], y2[1][:, :h])
+        y22 = (y2[0][:, h:], y2[1][:, h:])
+        g1 = halves(pair((ah_ref[:, :h], al_ref[:, :h]), y1, NT))
+        g2 = halves(pair((ah_ref[...], al_ref[...]), y2, NT))
+        e1 = (pair(y1, (g1[0][:h], g1[1][:h]), NN) - eye) * weight
+        e21 = pair(y2, g1, NN)
+        e22 = (pair(y2, g2, NN) - eye) * weight
+        worst = jnp.maximum(jnp.max(jnp.abs(e1)), jnp.maximum(jnp.max(jnp.abs(e21)), jnp.max(jnp.abs(e22))))
+        e1 = halves(e1)
+        e21 = halves(e21)
+        e22 = halves(e22)
+        y_ref[:h, :h] = y_ref[:h, :h] - pair(e1, y1, NN)
+        y_ref[h:, :h] = y_ref[h:, :h] - (pair(e21, y1, NN) + pair(e22, y21, NN))
+        y_ref[h:, h:] = y_ref[h:, h:] - pair(e22, y22, NN)
+        return step + 1, worst
 
     def unfinished(carry):
         step, worst = carry
-        return (step < 40) & jnp.logical_not(worst < 2e-3)
+        return (step < 40) & jnp.logical_not(worst < LIMIT)
 
     _, worst = lax.while_loop(unfinished, fine, (jnp.int32(0), jnp.float32(1.0)))
 
-    @pl.when(jnp.logical_not(worst < 2e-3))
+    @pl.when(jnp.logical_not(worst < LIMIT))
     def _():
-        w_ref[...] = a_ref[...]
-        y_ref[...] = eye
         row_id = lax.broadcasted_iota(jnp.int32, (n, 1), 0)
         col_id = lax.broadcasted_iota(jnp.int32, (1, n), 1)
+        w_ref[...] = a_ref[...]
+        y_ref[...] = jnp.where(row_id == col_id, 1.0, 0.0)
 
         def eliminate(k, carry):
             w = w_ref[...]
@@ -92,9 +124,9 @@
     block_row = lax.axis_index("leaf") % group
     block_col = lax.axis_index("front")
     pivots = n // b
-    y = y_ref[...]
-    xi = mm3(y, ai_ref[...], NN)
-    xj = mm3(y, aj_ref[...], NN)
+    y = halves(y_ref[...])
+    xi = pair(y, halves(ai_ref[...]), NN)
+    xj = pair(y, halves(aj_ref[...]), NN)
     schur = aij_ref[...] - mm3(xi, xj, TN)
     w_ref[:, :b] = xi
     picked = w_ref[pl.ds(pl.multiple_of(jnp.minimum(block_col, pivots - 1) * b, b), b), :b].T
@@ -113,10 +145,11 @@
         out_shape=jax.ShapeDtypeStruct((b, b), jnp.float32),
         in_specs=[vmem] * 4,
         out_specs=vmem,
-        scratch_shapes=[pltpu.VMEM((n, n), jnp.float32)] * 3,
+        scratch_shapes=[pltpu.VMEM((n, n), jnp.float32)] * 3 + [pltpu.VMEM((n, n), jnp.bfloat16)] * 2,
     )(corner, ai, aj, aij)
 
 PIV = 512
+LIMIT = 2e-3
 MESH = pl.DeviceIdType.MESH
 
 
@@ -127,7 +160,8 @@
     got_slice, got_block, piece, pieces,
     chunk_recv, chunk_plus, chunk_minus, chunk_twin, top_sem,
     slice_send, slice_recv, block_send, block_recv, piece_send, piece_recv,
-    plus_send, minus_send, twin_send, item_recv,
+    corner_top, row_top, corner_sum, row_sum,
+    top_send, top_recv, sum_send, sum_recv,
 ):
     blocks, b, _ = part_ref.shape
     pivots = corner_ref.shape[0]
@@ -188,7 +222,7 @@
         return (z + d + chips) % chips * 2 + core
 
     def reach(k):
-        return (half, half - 1) if k % 2 == 0 else (half - 1, half)
+        return (half, half - 1) if k % 2 else (half - 1, half)
 
     def launch(k):
         chunk_copy(k, front, chunk_plus, above).start()
@@ -242,33 +276,89 @@
 
         lax.fori_loop(0, blocks // 2, one, 0, unroll=True)
 
-    solve(0)
-    pl.semaphore_wait(barrier, group - 1 + 3)
-    launch(0)
-    solve(1)
-    launch(1)
-    for k in range(2, parts):
-        solve(k)
-    for d in range(1, half + 1):
-        for k in (0, 1):
-            relay(k, d)
-            if d == half - 1:
-                launch(k + 2)
-    twins(0)
-    relay(2, 1)
-    relay(3, 1)
-    gram(0)
-    relay(2, 2)
-    relay(3, 2)
-    twins(1)
-    gram(1)
-    for d in range(3, half + 1):
-        relay(2, d)
-        relay(3, d)
-    twins(2)
-    gram(2)
-    twins(3)
-    gram(3)
+    items = [(0, (p, q), q) for q in range(pivots) for p in range(q, pivots)]
+    items += [(1, (p,), me) for p in range(pivots)]
+    top_set = ((corner_top, row_top), top_send, top_recv)
+    sum_set = ((corner_sum, row_sum), sum_send, sum_recv)
+
+    def top_block(p):
+        return top_ref.at[p * b : (p + 1) * b, :]
+
+    def piece_block(p):
+        return pieces.at[p * b : (p + 1) * b, :]
+
+    def item_copy(chosen, n, src, way, to):
+        refs, send, recv = chosen
+        which, at, _ = items[n]
+        dst = refs[which].at[at]
+        return pltpu.make_async_remote_copy(
+            dst if src is None else src, dst, send.at[way, n], recv.at[n],
+            device_id=(leaf, to), device_id_type=MESH,
+        )
+
+    def roles(source):
+        lane = core == source % 2
+        far = (z + chips - source // 2) % chips
+        return lane, far, lane & (far < half), lane & ((far == 0) | (far > half + 1))
+
+    def items_launch(chosen, block):
+        for n, (which, at, source) in enumerate(items):
+            lane, far, plus, minus = roles(source)
+
+            @pl.when(lane & (far == 0))
+            def _():
+                src = block(at[0])
+                item_copy(chosen, n, src, 0, above).start()
+                item_copy(chosen, n, src, 1, below).start()
+                item_copy(chosen, n, src, 2, twin).start()
+                chosen[0][which][at] = src[...]
+
+    def relay_hop(t, chosen):
+        for n, (which, at, source) in enumerate(items):
+            lane, far, plus, minus = roles(source)
+
+            @pl.when(lane & (jnp.minimum(far, chips - far) == t))
+            def _():
+                item_copy(chosen, n, None, 2, twin).wait_recv()
+
+                @pl.when(plus)
+                def _():
+                    item_copy(chosen, n, None, 0, above).start()
+
+                @pl.when(minus)
+                def _():
+                    item_copy(chosen, n, None, 1, below).start()
+
+                item_copy(chosen, n, None, 2, twin).start()
+
+    def gather(window):
+        solve(0)
+        pl.semaphore_wait(barrier, group - 1 + 3)
+        launch(0)
+        for k in range(1, parts):
+            solve(k)
+            if k < window:
+                launch(k)
+        for first in range(0, parts, window):
+            last = first + window == parts
+            for d in range(1, half + 1):
+                for k in range(first, first + window):
+                    relay(k, d)
+                    if d == half - 1 and not last:
+                        launch(k + window)
+                    if d == half and last:
+                        if k == first:
+                            top_copy.wait()
+                            own_copy.wait()
+                            items_launch(top_set, top_block)
+                        twins(k)
+                        gram(k)
+                if first:
+                    for k in range(first - window, first)[d - 1 :: half]:
+                        twins(k)
+                        gram(k)
+
+    gather(2)
     for at in range(blocks):
         part_ref[at] = -acc[source(at)].astype(jnp.bfloat16)
 
@@ -287,7 +377,7 @@
 
     def piece_copy(to, src):
         return pltpu.make_async_remote_copy(
-            piece, pieces.at[src], piece_send.at[to], piece_recv.at[src],
+            piece, pieces.at[pl.ds(pl.multiple_of(src * rows, rows), rows), :], piece_send.at[to], piece_recv.at[src],
             device_id=(base + to, front), device_id_type=MESH,
         )
 
@@ -307,7 +397,7 @@
         return carry
 
     lax.fori_loop(1, group, send_slice, 0)
-    lax.fori_loop(1, group, send_block, 0)
+    relay_hop(1, top_set)
 
     def add_slice(d, total):
         src = other(d)
@@ -317,71 +407,40 @@
     mine = part_ref[me // per_block, pl.ds(pl.multiple_of(me % per_block * rows, rows), rows), :]
     total = lax.fori_loop(1, group, add_slice, mine.astype(jnp.float32))
     piece[...] = total.astype(jnp.bfloat16)
-    pieces[me] = total.astype(jnp.bfloat16)
+    pieces[pl.ds(pl.multiple_of(me * rows, rows), rows), :] = total.astype(jnp.bfloat16)
 
     def send_piece(d, carry):
         piece_copy(other(d), me).start()
         return carry
 
     lax.fori_loop(1, group, send_piece, 0)
+    lax.fori_loop(1, group, send_block, 0)
 
     def wait_piece(d, carry):
         src = other(d)
         piece_copy(src, src).wait_recv()
         return carry
 
+    relay_hop(2, top_set)
+    relay_hop(3, top_set)
     lax.fori_loop(1, group, wait_piece, 0)
-    top_copy.wait()
-    own_copy.wait()
+    relay_hop(half, top_set)
+    items_launch(sum_set, piece_block)
+    for t in range(1, half + 1):
+        relay_hop(t, sum_set)
+    for chosen in (top_set, sum_set):
+        for n in range(len(items)):
+
+            @pl.when(jnp.logical_not(roles(items[n][2])[0]))
+            def _():
+                item_copy(chosen, n, None, 2, twin).wait_recv()
+
     for p in range(pivots):
-        got = pieces[p * per_block : (p + 1) * per_block].astype(jnp.float32)
-        col_ref[p] = top_ref[p * b : (p + 1) * b, :] + got.reshape(b, b)
-
-    items = [(corner_ref, (p, q), q) for q in range(pivots) for p in range(q, pivots)]
-    items += [(row_ref, (p,), me) for p in range(pivots)]
-
-    def item_copy(n, sem, to):
-        ref, at, _ = items[n]
-        return pltpu.make_async_remote_copy(
-            ref.at[at], ref.at[at], sem.at[n], item_recv.at[n],
-            device_id=(leaf, to), device_id_type=MESH,
-        )
-
-    def roles(source):
-        lane = core == source % 2
-        far = (z + chips - source // 2) % chips
-        half = chips // 2
-        return lane, far, lane & (far < half), lane & ((far == 0) | (far > half + 1))
-
-    for n, (ref, at, source) in enumerate(items):
-        lane, far, plus, minus = roles(source)
-
-        @pl.when(lane & (far == 0))
-        def _():
-            ref[at] = col_ref[at[0]]
-
-        @pl.when(lane & (far != 0))
-        def _():
-            item_copy(n, twin_send, twin).wait_recv()
-
-        @pl.when(plus)
-        def _():
-            item_copy(n, plus_send, above).start()
-
-        @pl.when(minus)
-        def _():
-            item_copy(n, minus_send, below).start()
-
-        @pl.when(lane)
-        def _():
-            item_copy(n, twin_send, twin).start()
-
-    for n, (ref, at, source) in enumerate(items):
-        lane, far, plus, minus = roles(source)
-
-        @pl.when(jnp.logical_not(lane))
-        def _():
-            item_copy(n, twin_send, twin).wait_recv()
+        rows_p = slice(p * b, (p + 1) * b)
+        col_ref[p] = top_ref[rows_p, :] + pieces[rows_p, :].astype(jnp.float32)
+        row_ref[p] = row_top[p] + row_sum[p].astype(jnp.float32)
+        for q in range(p + 1):
+            corner_ref[p, q] = corner_top[p, q] + corner_sum[p, q].astype(jnp.float32)
 
     own_ref[...] = block_ref[...] + part_ref[me].astype(jnp.float32)
 
@@ -407,20 +466,21 @@
         return carry
 
     lax.fori_loop(1, group, drain, 0)
-    for n, (ref, at, source) in enumerate(items):
-        lane, far, plus, minus = roles(source)
-
-        @pl.when(plus)
-        def _():
-            item_copy(n, plus_send, above).wait_send()
-
-        @pl.when(minus)
-        def _():
-            item_copy(n, minus_send, below).wait_send()
-
-        @pl.when(lane)
-        def _():
-            item_copy(n, twin_send, twin).wait_send()
+    for chosen in (top_set, sum_set):
+        for n in range(len(items)):
+            lane, far, plus, minus = roles(items[n][2])
+
+            @pl.when(plus)
+            def _():
+                item_copy(chosen, n, None, 0, above).wait_send()
+
+            @pl.when(minus)
+            def _():
+                item_copy(chosen, n, None, 1, below).wait_send()
+
+            @pl.when(lane)
+            def _():
+                item_copy(chosen, n, None, 2, twin).wait_send()
 
     for k in range(parts):
         up, down = reach(k)
@@ -468,12 +528,18 @@
             pltpu.VMEM((group, rows, b), bf16),
             pltpu.VMEM((group, b, b), bf16),
             pltpu.VMEM((rows, b), bf16),
-            pltpu.VMEM((group, rows, b), bf16),
+            pltpu.VMEM((PIV, b), bf16),
         ]
         + [dma((parts, blocks))] * 4
         + [dma((2,))]
         + [dma((group,))] * 6
-        + [dma((items,))] * 4,
+        + [
+            pltpu.VMEM((pivots, pivots, b, b), f32),
+            pltpu.VMEM((pivots, b, b), f32),
+            pltpu.VMEM((pivots, pivots, b, b), bf16),
+            pltpu.VMEM((pivots, b, b), bf16),
+        ]
+        + [dma((3, items)), dma((items,))] * 2,
         compiler_params=pltpu.CompilerParams(collective_id=1, has_side_effects=True),
     )(coupling, factors, tops, pattern, sizes, maps)
 

time: 131 us -> 112 us (0.85)
  Pallas kernels: 129 us -> 110 us
    pallas_call x1, Pallas kernels: 117 us -> 101 us  [assemble(): pl.pallas_call(functools.partial(assemble_kernel, group, chips), out_shap...]
    pallas_call x1, Pallas kernels: 11.3 us -> 8.96 us  [finish(): pl.pallas_call(functools.partial(finish_kernel, group), out_shape=jax.Sha...]
where the time goes in v5:
time: 112 us
  Pallas kernels  110 us (98%)
  local copies, waits for them, and re-layouts  1.33 us (1%)
    pallas_call x1, Pallas kernels, assemble(): pl.pallas_call(functools.partial(assemble_kernel, group, chips), out_shap...  101 us
    pallas_call x1, Pallas kernels, finish(): pl.pallas_call(functools.partial(finish_kernel, group), out_shape=jax.Sha...  8.96 us

profile of v5, /device:TPU:7, one launch (start us, length us, event | category | flops | bytes accessed | tf_op | source)
XLA Modules:
  0.0 112.1 jit_solution(7825193063224295007)
XLA Ops:
  0.7 1.3 %copy.7.pattern_ref = s32[1,16,1]{2,1,0:T(8,128)} copy(s32[1,16,1]{1,2,0:T(1,128)} %param.7) | data formatting | bytes 128 | tf_op args[1]
  2.0 101.2 %shard_map.64 = (f32[128,128]{1,0:T(8,128)}, f32[4,4,128,128]{3,2,1,0:T(8,128)}, f32[4,128,128]{2,1,0:T(8,128)}, f32[4,128,128]{2,1,0:T(8,128)}) custom-call(bf16[2048,128]{1,0:T(8,128)(2,1)} %coupling_ref.1, bf16[16,128,128]{2,1,0:T(8,128)(2,1)} %factor_ref.1, f32[2,2048,128]{2,1,0:T(8,128)} %tops_ref.1, s32[1,16,1]{2,1,0:T(8,128)} %copy.7.pattern_ref, ...), custom_call_target="tpu_custom_call" | custom-call | tf_op jit(solution)/shard_map/pallas_call | solution.py:512
  103.2 9.0 %shard_map.65 = f32[128,128]{1,0:T(8,128)} custom-call(f32[4,4,128,128]{3,2,1,0:T(8,128)} %get-tuple-element.9.corner_ref, f32[512,128]{1,0:T(8,128)} %bitcast.2, f32[512,128]{1,0:T(8,128)} %bitcast.3, f32[128,128]{1,0:T(8,128)} %get-tuple-element.12.aij_ref), custom_call_target="tpu_custom_call" | custom-call | tf_op jit(solution)/shard_map/pallas_call | solution.py:143

commit v6 on v5

--- a/solution.py
+++ b/solution.py
@@ -83,7 +83,7 @@
         e1 = (pair(y1, (g1[0][:h], g1[1][:h]), NN) - eye) * weight
         e21 = pair(y2, g1, NN)
         e22 = (pair(y2, g2, NN) - eye) * weight
-        worst = jnp.maximum(jnp.max(jnp.abs(e1)), jnp.maximum(jnp.max(jnp.abs(e21)), jnp.max(jnp.abs(e22))))
+        worst = jnp.sum(e1 * e1) + jnp.sum(e21 * e21) + jnp.sum(e22 * e22)
         e1 = halves(e1)
         e21 = halves(e21)
         e22 = halves(e22)
@@ -149,13 +149,14 @@
     )(corner, ai, aj, aij)
 
 PIV = 512
-LIMIT = 2e-3
+LIMIT = 4e-3
 MESH = pl.DeviceIdType.MESH
 
 
 def assemble_kernel(
-    group, chips, coupling_ref, factor_ref, tops_ref, pattern_ref, size_ref, map_ref,
+    group, chips, coupling_hbm, factor_hbm, tops_ref, pattern_ref, size_ref, map_ref,
     own_ref, corner_ref, row_ref, col_ref,
+    coupling_ref, factor_ref, in_sem,
     bufs, acc, part_ref, top_ref, block_ref,
     got_slice, got_block, piece, pieces,
     chunk_recv, chunk_plus, chunk_minus, chunk_twin, top_sem,
@@ -180,6 +181,26 @@
     def other(d):
         return (me + d) % group
 
+    parts = len(bufs)
+    supers = factor_ref.shape[0] // parts
+
+    def input_copies(k):
+        first = k * supers
+        return (
+            pltpu.make_async_copy(
+                coupling_hbm.at[pl.ds(first * b, supers * b), :],
+                coupling_ref.at[pl.ds(first * b, supers * b), :],
+                in_sem.at[0, k],
+            ),
+            pltpu.make_async_copy(
+                factor_hbm.at[pl.ds(first, supers)], factor_ref.at[pl.ds(first, supers)],
+                in_sem.at[1, k],
+            ),
+        )
+
+    for k in range(parts):
+        for copy in input_copies(k):
+            copy.start()
     top_copy = pltpu.make_async_copy(
         tops_ref.at[leaf // group, pl.ds(0, pivots * b), :], top_ref, top_sem.at[0]
     )
@@ -199,16 +220,16 @@
     for side in (twin, above, below):
         pl.semaphore_signal(barrier, 1, device_id=(leaf, side), device_id_type=MESH)
 
-    parts = len(bufs)
-    supers = factor_ref.shape[0] // parts
     half = chips // 2
     row_id = lax.broadcasted_iota(jnp.int32, (b, b), 0)
 
     def solve(k):
+        for copy in input_copies(k):
+            copy.wait()
         for r in range(supers):
             n = k * supers + r
             solved = mm(factor_ref[n], coupling_ref[n * b : (n + 1) * b, :], NN)
-            live = jnp.where(row_id + n * b < size_ref[0], pattern_ref[0, n, 0], 0)
+            live = jnp.where(row_id + n * b < size_ref[0], pattern_ref[0, 0, n], 0)
             kept = jnp.where(live > 0, solved, 0.0)
             bufs[k][front, :, r * b : (r + 1) * b] = kept.T.astype(jnp.bfloat16)
 
@@ -424,9 +445,10 @@
     relay_hop(2, top_set)
     relay_hop(3, top_set)
     lax.fori_loop(1, group, wait_piece, 0)
+    items_launch(sum_set, piece_block)
+    relay_hop(1, sum_set)
     relay_hop(half, top_set)
-    items_launch(sum_set, piece_block)
-    for t in range(1, half + 1):
+    for t in range(2, half + 1):
         relay_hop(t, sum_set)
     for chosen in (top_set, sum_set):
         for n in range(len(items)):
@@ -517,9 +539,12 @@
             jax.ShapeDtypeStruct((pivots, b, b), f32),
             jax.ShapeDtypeStruct((pivots, b, b), f32),
         ),
-        in_specs=[vmem] * 2 + [pl.BlockSpec(memory_space=pl.ANY)] + [smem] * 3,
+        in_specs=[pl.BlockSpec(memory_space=pltpu.MemorySpace.HBM)] * 3 + [smem] * 3,
         out_specs=[vmem] * 4,
         scratch_shapes=[
+            pltpu.VMEM(coupling.shape, bf16),
+            pltpu.VMEM(factors.shape, bf16),
+            dma((2, parts)),
             [pltpu.VMEM((blocks, b, coupling.shape[0] // parts), bf16)] * parts,
             pltpu.VMEM((blocks, b, b), f32),
             pltpu.VMEM((blocks, b, b), bf16),
@@ -549,7 +574,7 @@
     chips = lax.axis_size("front") // 2
     own, corner, own_row, own_col = assemble(
         group, chips, coupling, supernode_inverse, top_fronts,
-        block_pattern, subdomain_sizes, block_maps,
+        block_pattern.transpose(0, 2, 1), subdomain_sizes, block_maps,
     )
     flat = (PIV, coupling.shape[1])
     return finish(group, corner, own_row.reshape(flat), own_col.reshape(flat), own)

time: 112 us -> 103 us (0.920)
  Pallas kernels: 110 us -> 102 us
  local copies, waits for them, and re-layouts: 1.33 us -> 0 us
    pallas_call x1, Pallas kernels: 101 us -> 95 us  [assemble(): pl.pallas_call(functools.partial(assemble_kernel, group, chips), out_shap...]
    pallas_call x1, Pallas kernels: 8.96 us -> 7.09 us  [finish(): pl.pallas_call(functools.partial(finish_kernel, group), out_shape=jax.Sha...]
    unnamed x1 -> x0, local copies, waits for them, and re-layouts: 1.33 us -> none
where the time goes in v6:
time: 103 us
  Pallas kernels  102 us (99%)
    pallas_call x1, Pallas kernels, assemble(): pl.pallas_call(functools.partial(assemble_kernel, group, chips), out_shap...  95 us
    pallas_call x1, Pallas kernels, finish(): pl.pallas_call(functools.partial(finish_kernel, group), out_shape=jax.Sha...  7.09 us

profile of v6, /device:TPU:7, one launch (start us, length us, event | category | flops | bytes accessed | tf_op | source)
XLA Modules:
  0.0 102.8 jit_solution(4958508232175399161)
XLA Ops:
  0.7 95.0 %shard_map.64 = (f32[128,128]{1,0:T(8,128)}, f32[4,4,128,128]{3,2,1,0:T(8,128)}, f32[4,128,128]{2,1,0:T(8,128)}, f32[4,128,128]{2,1,0:T(8,128)}) custom-call(bf16[2048,128]{1,0:T(8,128)(2,1)} %coupling_hbm.1, bf16[16,128,128]{2,1,0:T(8,128)(2,1)} %factor_hbm.1, f32[2,2048,128]{2,1,0:T(8,128)} %tops_ref.1, s32[1,1,16]{2,1,0:T(1,128)} %bitcast.5, ...), custom_call_target="tpu_custom_call" | custom-call | tf_op jit(solution)/shard_map/pallas_call | solution.py:534
  95.7 7.1 %shard_map.65 = f32[128,128]{1,0:T(8,128)} custom-call(f32[4,4,128,128]{3,2,1,0:T(8,128)} %get-tuple-element.9.corner_ref, f32[512,128]{1,0:T(8,128)} %bitcast.3, f32[512,128]{1,0:T(8,128)} %bitcast.4, f32[128,128]{1,0:T(8,128)} %get-tuple-element.12.aij_ref), custom_call_target="tpu_custom_call" | custom-call | tf_op jit(solution)/shard_map/pallas_call | solution.py:143

commit v7 on v6

--- a/solution.py
+++ b/solution.py
@@ -33,7 +33,7 @@
     b = ai_ref.shape[1]
     for p in range(n // b):
         for q in range(p + 1):
-            block = corner_ref[p, q]
+            block = corner_ref[p * (p + 1) // 2 + q]
             a_ref[p * b : (p + 1) * b, q * b : (q + 1) * b] = block
             if q < p:
                 a_ref[q * b : (q + 1) * b, p * b : (p + 1) * b] = block.T
@@ -165,7 +165,7 @@
     top_send, top_recv, sum_send, sum_recv,
 ):
     blocks, b, _ = part_ref.shape
-    pivots = corner_ref.shape[0]
+    pivots = row_ref.shape[0]
     rows = piece.shape[0]
     per_block = b // rows
     leaf = lax.axis_index("leaf")
@@ -373,15 +373,19 @@
                             own_copy.wait()
                             items_launch(top_set, top_block)
                         twins(k)
-                        gram(k)
+                        if k < parts - 1:
+                            gram(k)
                 if first:
                     for k in range(first - window, first)[d - 1 :: half]:
                         twins(k)
                         gram(k)
 
     gather(2)
-    for at in range(blocks):
-        part_ref[at] = -acc[source(at)].astype(jnp.bfloat16)
+    final = parts - 1
+    picked = bufs[final][source(front)]
+    for at in range(pivots):
+        found = source(at)
+        part_ref[at] = -(acc[found] + mm(bufs[final][found], picked, NT)).astype(jnp.bfloat16)
 
     def slice_copy(to, src):
         return pltpu.make_async_remote_copy(
@@ -418,6 +422,9 @@
         return carry
 
     lax.fori_loop(1, group, send_slice, 0)
+    gram(final)
+    for at in range(pivots, blocks):
+        part_ref[at] = -acc[source(at)].astype(jnp.bfloat16)
     relay_hop(1, top_set)
 
     def add_slice(d, total):
@@ -446,9 +453,9 @@
     relay_hop(3, top_set)
     lax.fori_loop(1, group, wait_piece, 0)
     items_launch(sum_set, piece_block)
-    relay_hop(1, sum_set)
-    relay_hop(half, top_set)
-    for t in range(2, half + 1):
+    for t in range(1, half + 1):
+        if t == half:
+            relay_hop(half, top_set)
         relay_hop(t, sum_set)
     for chosen in (top_set, sum_set):
         for n in range(len(items)):
@@ -462,7 +469,7 @@
         col_ref[p] = top_ref[rows_p, :] + pieces[rows_p, :].astype(jnp.float32)
         row_ref[p] = row_top[p] + row_sum[p].astype(jnp.float32)
         for q in range(p + 1):
-            corner_ref[p, q] = corner_top[p, q] + corner_sum[p, q].astype(jnp.float32)
+            corner_ref[p * (p + 1) // 2 + q] = corner_top[p, q] + corner_sum[p, q].astype(jnp.float32)
 
     own_ref[...] = block_ref[...] + part_ref[me].astype(jnp.float32)
 
@@ -535,7 +542,7 @@
         functools.partial(assemble_kernel, group, chips),
         out_shape=(
             jax.ShapeDtypeStruct((b, b), f32),
-            jax.ShapeDtypeStruct((pivots, pivots, b, b), f32),
+            jax.ShapeDtypeStruct((pivots * (pivots + 1) // 2, b, b), f32),
             jax.ShapeDtypeStruct((pivots, b, b), f32),
             jax.ShapeDtypeStruct((pivots, b, b), f32),
         ),

time: 103 us -> 102 us (level)
  no operation moved by 1% of the time
where the time goes in v7:
time: 102 us
  Pallas kernels  101 us (99%)
    pallas_call x1, Pallas kernels, assemble(): pl.pallas_call(functools.partial(assemble_kernel, group, chips), out_shap...  94.2 us
    pallas_call x1, Pallas kernels, finish(): pl.pallas_call(functools.partial(finish_kernel, group), out_shape=jax.Sha...  6.97 us

profile of v7, /device:TPU:7, one launch (start us, length us, event | category | flops | bytes accessed | tf_op | source)
XLA Modules:
  0.0 101.9 jit_solution(16108469885844225034)
XLA Ops:
  0.7 94.2 %shard_map.64 = (f32[128,128]{1,0:T(8,128)}, f32[10,128,128]{2,1,0:T(8,128)}, f32[4,128,128]{2,1,0:T(8,128)}, f32[4,128,128]{2,1,0:T(8,128)}) custom-call(bf16[2048,128]{1,0:T(8,128)(2,1)} %coupling_hbm.1, bf16[16,128,128]{2,1,0:T(8,128)(2,1)} %factor_hbm.1, f32[2,2048,128]{2,1,0:T(8,128)} %tops_ref.1, s32[1,1,16]{2,1,0:T(1,128)} %bitcast.5, ...), custom_call_target="tpu_custom_call" | custom-call | tf_op jit(solution)/shard_map/pallas_call | solution.py:541
  94.9 7.0 %shard_map.65 = f32[128,128]{1,0:T(8,128)} custom-call(f32[10,128,128]{2,1,0:T(8,128)} %get-tuple-element.9.corner_ref, f32[512,128]{1,0:T(8,128)} %bitcast.3, f32[512,128]{1,0:T(8,128)} %bitcast.4, f32[128,128]{1,0:T(8,128)} %get-tuple-element.12.aij_ref), custom_call_target="tpu_custom_call" | custom-call | tf_op jit(solution)/shard_map/pallas_call | solution.py:143

commit v8 on v7

--- a/solution.py
+++ b/solution.py
@@ -76,20 +76,20 @@
         step, _ = carry
         y1 = halves(y_ref[:h, :h])
         y2 = halves(y_ref[h:, :])
-        y21 = (y2[0][:, :h], y2[1][:, :h])
-        y22 = (y2[0][:, h:], y2[1][:, h:])
+        y21 = y2[0][:, :h]
+        y22 = y2[0][:, h:]
         g1 = halves(pair((ah_ref[:, :h], al_ref[:, :h]), y1, NT))
         g2 = halves(pair((ah_ref[...], al_ref[...]), y2, NT))
         e1 = (pair(y1, (g1[0][:h], g1[1][:h]), NN) - eye) * weight
         e21 = pair(y2, g1, NN)
         e22 = (pair(y2, g2, NN) - eye) * weight
         worst = jnp.sum(e1 * e1) + jnp.sum(e21 * e21) + jnp.sum(e22 * e22)
-        e1 = halves(e1)
-        e21 = halves(e21)
-        e22 = halves(e22)
-        y_ref[:h, :h] = y_ref[:h, :h] - pair(e1, y1, NN)
-        y_ref[h:, :h] = y_ref[h:, :h] - (pair(e21, y1, NN) + pair(e22, y21, NN))
-        y_ref[h:, h:] = y_ref[h:, h:] - pair(e22, y22, NN)
+        e1 = e1.astype(jnp.bfloat16)
+        e21 = e21.astype(jnp.bfloat16)
+        e22 = e22.astype(jnp.bfloat16)
+        y_ref[:h, :h] = y_ref[:h, :h] - mm(e1, y1[0], NN)
+        y_ref[h:, :h] = y_ref[h:, :h] - (mm(e21, y1[0], NN) + mm(e22, y21, NN))
+        y_ref[h:, h:] = y_ref[h:, h:] - mm(e22, y22, NN)
         return step + 1, worst
 
     def unfinished(carry):
@@ -124,11 +124,14 @@
     block_row = lax.axis_index("leaf") % group
     block_col = lax.axis_index("front")
     pivots = n // b
-    y = halves(y_ref[...])
-    xi = pair(y, halves(ai_ref[...]), NN)
-    xj = pair(y, halves(aj_ref[...]), NN)
-    schur = aij_ref[...] - mm3(xi, xj, TN)
-    w_ref[:, :b] = xi
+    w_ref[:, :b] = ai_ref[...]
+    w_ref[:, b : 2 * b] = aj_ref[...]
+    right_h, right_l = halves(w_ref[:, : 2 * b])
+    y1 = halves(y_ref[:h, :h])
+    y2 = halves(y_ref[h:, :])
+    w_ref[:h, : 2 * b] = pair(y1, (right_h[:h], right_l[:h]), NN)
+    w_ref[h:, : 2 * b] = pair(y2, (right_h, right_l), NN)
+    schur = aij_ref[...] - mm3(w_ref[:, :b], w_ref[:, b : 2 * b], TN)
     picked = w_ref[pl.ds(pl.multiple_of(jnp.minimum(block_col, pivots - 1) * b, b), b), :b].T
     r = block_row * b + lax.broadcasted_iota(jnp.int32, (b, b), 0)
     c = block_col * b + lax.broadcasted_iota(jnp.int32, (b, b), 1)
@@ -150,6 +153,8 @@
 
 PIV = 512
 LIMIT = 4e-3
+CHUNKS = (4, 4, 4, 4)
+EARLY = 6
 MESH = pl.DeviceIdType.MESH
 
 
@@ -182,10 +187,10 @@
         return (me + d) % group
 
     parts = len(bufs)
-    supers = factor_ref.shape[0] // parts
+    firsts = [sum(CHUNKS[:k]) for k in range(parts)]
 
     def input_copies(k):
-        first = k * supers
+        first, supers = firsts[k], CHUNKS[k]
         return (
             pltpu.make_async_copy(
                 coupling_hbm.at[pl.ds(first * b, supers * b), :],
@@ -226,8 +231,8 @@
     def solve(k):
         for copy in input_copies(k):
             copy.wait()
-        for r in range(supers):
-            n = k * supers + r
+        for r in range(CHUNKS[k]):
+            n = firsts[k] + r
             solved = mm(factor_ref[n], coupling_ref[n * b : (n + 1) * b, :], NN)
             live = jnp.where(row_id + n * b < size_ref[0], pattern_ref[0, 0, n], 0)
             kept = jnp.where(live > 0, solved, 0.0)
@@ -425,6 +430,7 @@
     gram(final)
     for at in range(pivots, blocks):
         part_ref[at] = -acc[source(at)].astype(jnp.bfloat16)
+    lax.fori_loop(1, EARLY, send_block, 0)
     relay_hop(1, top_set)
 
     def add_slice(d, total):
@@ -442,7 +448,7 @@
         return carry
 
     lax.fori_loop(1, group, send_piece, 0)
-    lax.fori_loop(1, group, send_block, 0)
+    lax.fori_loop(EARLY, group, send_block, 0)
 
     def wait_piece(d, carry):
         src = other(d)
@@ -532,7 +538,7 @@
     pivots = PIV // b
     rows = PIV // group
     items = pivots * (pivots + 1) // 2 + pivots
-    parts = 4
+    parts = len(CHUNKS)
     vmem = pl.BlockSpec(memory_space=pltpu.VMEM)
     smem = pl.BlockSpec(memory_space=pltpu.SMEM)
     dma = pltpu.SemaphoreType.DMA
@@ -552,7 +558,7 @@
             pltpu.VMEM(coupling.shape, bf16),
             pltpu.VMEM(factors.shape, bf16),
             dma((2, parts)),
-            [pltpu.VMEM((blocks, b, coupling.shape[0] // parts), bf16)] * parts,
+            [pltpu.VMEM((blocks, b, size * b), bf16) for size in CHUNKS],
             pltpu.VMEM((blocks, b, b), f32),
             pltpu.VMEM((blocks, b, b), bf16),
             pltpu.VMEM((PIV, b), f32),

time: 102 us -> 102 us (level)
  no operation moved by 1% of the time
where the time goes in v8:
time: 102 us; the launch traced here: 101 us
  Pallas kernels  101 us (99%)
    pallas_call x1, Pallas kernels, assemble(): pl.pallas_call(functools.partial(assemble_kernel, group, chips), out_shap...  94.3 us
    pallas_call x1, Pallas kernels, finish(): pl.pallas_call(functools.partial(finish_kernel, group), out_shape=jax.Sha...  6.48 us

profile of v8, /device:TPU:7, one launch (start us, length us, event | category | flops | bytes accessed | tf_op | source)
XLA Modules:
  0.0 101.4 jit_solution(6543173971656761774)
XLA Ops:
  0.7 94.3 %shard_map.64 = (f32[128,128]{1,0:T(8,128)}, f32[10,128,128]{2,1,0:T(8,128)}, f32[4,128,128]{2,1,0:T(8,128)}, f32[4,128,128]{2,1,0:T(8,128)}) custom-call(bf16[2048,128]{1,0:T(8,128)(2,1)} %coupling_hbm.1, bf16[16,128,128]{2,1,0:T(8,128)(2,1)} %factor_hbm.1, f32[2,2048,128]{2,1,0:T(8,128)} %tops_ref.1, s32[1,1,16]{2,1,0:T(1,128)} %bitcast.5, ...), custom_call_target="tpu_custom_call" | custom-call | tf_op jit(solution)/shard_map/pallas_call | solution.py:547
  94.9 6.5 %shard_map.65 = f32[128,128]{1,0:T(8,128)} custom-call(f32[10,128,128]{2,1,0:T(8,128)} %get-tuple-element.9.corner_ref, f32[512,128]{1,0:T(8,128)} %bitcast.3, f32[512,128]{1,0:T(8,128)} %bitcast.4, f32[128,128]{1,0:T(8,128)} %get-tuple-element.12.aij_ref), custom_call_target="tpu_custom_call" | custom-call | tf_op jit(solution)/shard_map/pallas_call | solution.py:146

commit v9 on v8

--- a/solution.py
+++ b/solution.py
@@ -153,7 +153,7 @@
 
 PIV = 512
 LIMIT = 4e-3
-CHUNKS = (4, 4, 4, 4)
+CHUNKS = (8, 8)
 EARLY = 6
 MESH = pl.DeviceIdType.MESH
 
@@ -459,24 +459,8 @@
     relay_hop(3, top_set)
     lax.fori_loop(1, group, wait_piece, 0)
     items_launch(sum_set, piece_block)
-    for t in range(1, half + 1):
-        if t == half:
-            relay_hop(half, top_set)
+    for t in range(1, half):
         relay_hop(t, sum_set)
-    for chosen in (top_set, sum_set):
-        for n in range(len(items)):
-
-            @pl.when(jnp.logical_not(roles(items[n][2])[0]))
-            def _():
-                item_copy(chosen, n, None, 2, twin).wait_recv()
-
-    for p in range(pivots):
-        rows_p = slice(p * b, (p + 1) * b)
-        col_ref[p] = top_ref[rows_p, :] + pieces[rows_p, :].astype(jnp.float32)
-        row_ref[p] = row_top[p] + row_sum[p].astype(jnp.float32)
-        for q in range(p + 1):
-            corner_ref[p * (p + 1) // 2 + q] = corner_top[p, q] + corner_sum[p, q].astype(jnp.float32)
-
     own_ref[...] = block_ref[...] + part_ref[me].astype(jnp.float32)
 
     @pl.when(inner & (me >= pivots))
@@ -488,6 +472,22 @@
             return carry
 
         lax.fori_loop(1, group, add_block, 0)
+
+    relay_hop(half, top_set)
+    relay_hop(half, sum_set)
+    for chosen in (top_set, sum_set):
+        for n in range(len(items)):
+
+            @pl.when(jnp.logical_not(roles(items[n][2])[0]))
+            def _():
+                item_copy(chosen, n, None, 2, twin).wait_recv()
+
+    for p in range(pivots):
+        rows_p = slice(p * b, (p + 1) * b)
+        col_ref[p] = top_ref[rows_p, :] + pieces[rows_p, :].astype(jnp.float32)
+        row_ref[p] = row_top[p] + row_sum[p].astype(jnp.float32)
+        for q in range(p + 1):
+            corner_ref[p * (p + 1) // 2 + q] = corner_top[p, q] + corner_sum[p, q].astype(jnp.float32)
 
     def drain(d, carry):
         to = other(d)

time: 102 us -> 100 us (0.980)
  Pallas kernels: 101 us -> 99.2 us
    pallas_call x1, Pallas kernels: 94.3 us -> 92.8 us  [assemble(): pl.pallas_call(functools.partial(assemble_kernel, group, chips), out_shap...]
where the time goes in v9:
time: 100 us; the launch traced here: 99.9 us
  Pallas kernels  99.2 us (99%)
    pallas_call x1, Pallas kernels, assemble(): pl.pallas_call(functools.partial(assemble_kernel, group, chips), out_shap...  92.8 us
    pallas_call x1, Pallas kernels, finish(): pl.pallas_call(functools.partial(finish_kernel, group), out_shape=jax.Sha...  6.48 us

profile of v9, /device:TPU:7, one launch (start us, length us, event | category | flops | bytes accessed | tf_op | source)
XLA Modules:
  0.0 99.9 jit_solution(7721719316106634565)
XLA Ops:
  0.7 92.8 %shard_map.64 = (f32[128,128]{1,0:T(8,128)}, f32[10,128,128]{2,1,0:T(8,128)}, f32[4,128,128]{2,1,0:T(8,128)}, f32[4,128,128]{2,1,0:T(8,128)}) custom-call(bf16[2048,128]{1,0:T(8,128)(2,1)} %coupling_hbm.1, bf16[16,128,128]{2,1,0:T(8,128)(2,1)} %factor_hbm.1, f32[2,2048,128]{2,1,0:T(8,128)} %tops_ref.1, s32[1,1,16]{2,1,0:T(1,128)} %bitcast.5, ...), custom_call_target="tpu_custom_call" | custom-call | tf_op jit(solution)/shard_map/pallas_call | solution.py:547
  93.4 6.5 %shard_map.65 = f32[128,128]{1,0:T(8,128)} custom-call(f32[10,128,128]{2,1,0:T(8,128)} %get-tuple-element.9.corner_ref, f32[512,128]{1,0:T(8,128)} %bitcast.3, f32[512,128]{1,0:T(8,128)} %bitcast.4, f32[128,128]{1,0:T(8,128)} %get-tuple-element.12.aij_ref), custom_call_target="tpu_custom_call" | custom-call | tf_op jit(solution)/shard_map/pallas_call | solution.py:146

commit v10 on v9

--- a/solution.py
+++ b/solution.py
@@ -27,10 +27,20 @@
     return mm(ah, bh, dims) + (mm(ah, bl, dims) + mm(al, bh, dims))
 
 
-def finish_kernel(group, corner_ref, ai_ref, aj_ref, aij_ref, out_ref, a_ref, y_ref, w_ref, ah_ref, al_ref):
+def finish_kernel(
+    group, corner_ref, ai_hbm, aj_hbm, aij_hbm, out_ref,
+    a_ref, y_ref, w_ref, ah_ref, al_ref, side_ref, aij_ref, side_sem,
+):
     n = a_ref.shape[0]
     h = n // 2
-    b = ai_ref.shape[1]
+    b = ai_hbm.shape[1]
+    side_copies = (
+        pltpu.make_async_copy(ai_hbm, side_ref.at[0], side_sem.at[0]),
+        pltpu.make_async_copy(aj_hbm, side_ref.at[1], side_sem.at[1]),
+        pltpu.make_async_copy(aij_hbm, aij_ref, side_sem.at[2]),
+    )
+    for copy in side_copies:
+        copy.start()
     for p in range(n // b):
         for q in range(p + 1):
             block = corner_ref[p * (p + 1) // 2 + q]
@@ -124,8 +134,10 @@
     block_row = lax.axis_index("leaf") % group
     block_col = lax.axis_index("front")
     pivots = n // b
-    w_ref[:, :b] = ai_ref[...]
-    w_ref[:, b : 2 * b] = aj_ref[...]
+    for copy in side_copies:
+        copy.wait()
+    w_ref[:, :b] = side_ref[0]
+    w_ref[:, b : 2 * b] = side_ref[1]
     right_h, right_l = halves(w_ref[:, : 2 * b])
     y1 = halves(y_ref[:h, :h])
     y2 = halves(y_ref[h:, :])
@@ -146,9 +158,10 @@
     return pl.pallas_call(
         functools.partial(finish_kernel, group),
         out_shape=jax.ShapeDtypeStruct((b, b), jnp.float32),
-        in_specs=[vmem] * 4,
+        in_specs=[vmem] + [pl.BlockSpec(memory_space=pl.ANY)] * 3,
         out_specs=vmem,
-        scratch_shapes=[pltpu.VMEM((n, n), jnp.float32)] * 3 + [pltpu.VMEM((n, n), jnp.bfloat16)] * 2,
+        scratch_shapes=[pltpu.VMEM((n, n), jnp.float32)] * 3 + [pltpu.VMEM((n, n), jnp.bfloat16)] * 2
+        + [pltpu.VMEM((2, n, b), jnp.float32), pltpu.VMEM((b, b), jnp.float32), pltpu.SemaphoreType.DMA((3,))],
     )(corner, ai, aj, aij)
 
 PIV = 512

time: 100 us -> 100 us (level)
  no operation moved by 1% of the time
where the time goes in v10:
time: 100 us; the launch traced here: 99.8 us
  Pallas kernels  99.1 us (99%)
    pallas_call x1, Pallas kernels, assemble(): pl.pallas_call(functools.partial(assemble_kernel, group, chips), out_shap...  92.8 us
    pallas_call x1, Pallas kernels, finish(): pl.pallas_call(functools.partial(finish_kernel, group), out_shape=jax.Sha...  6.38 us

profile of v10, /device:TPU:7, one launch (start us, length us, event | category | flops | bytes accessed | tf_op | source)
XLA Modules:
  0.0 99.8 jit_solution(323379174646723307)
XLA Ops:
  0.7 92.8 %shard_map.64 = (f32[128,128]{1,0:T(8,128)}, f32[10,128,128]{2,1,0:T(8,128)}, f32[4,128,128]{2,1,0:T(8,128)}, f32[4,128,128]{2,1,0:T(8,128)}) custom-call(bf16[2048,128]{1,0:T(8,128)(2,1)} %coupling_hbm.1, bf16[16,128,128]{2,1,0:T(8,128)(2,1)} %factor_hbm.1, f32[2,2048,128]{2,1,0:T(8,128)} %tops_ref.1, s32[1,1,16]{2,1,0:T(1,128)} %bitcast.5, ...), custom_call_target="tpu_custom_call" | custom-call | tf_op jit(solution)/shard_map/pallas_call | solution.py:560
  93.4 6.4 %shard_map.65 = f32[128,128]{1,0:T(8,128)} custom-call(f32[10,128,128]{2,1,0:T(8,128)} %get-tuple-element.9.corner_ref, f32[512,128]{1,0:T(8,128)} %bitcast.3, f32[512,128]{1,0:T(8,128)} %bitcast.4, f32[128,128]{1,0:T(8,128)} %get-tuple-element.12.aij_hbm), custom_call_target="tpu_custom_call" | custom-call | tf_op jit(solution)/shard_map/pallas_call | solution.py:158
